TPU v7x, 32 devices: a whole 2x2x4 slice. The times are simulated.
32 devices in a mesh: prow: 8 (over z, y), pcol: 4 (over x, core).
Axes of the slice: x: 2, y: 2, z: 4, core: 2. Of those that a mesh axis runs over, the one named last changes fastest.
Arguments:
- ainv: bfloat16 [3, 8, 256, 6, 4, 256], P(None, 'prow', None, None, 'pcol'), may hold values from -0.078125 to 0.078125
- panel: bfloat16 [6, 4, 256, 1536], P(None, 'pcol', None, 'prow'), may hold values from -6 to 6
- structure: int32 [4, 24], replicated, may hold values 0 or 1
- widths: int32 [4], replicated, may hold values from 1 to 512, 1536 in all
Outputs:
- inverse_panel: bfloat16 [3, 8, 256, 1536], P(None, 'prow', None, 'pcol')
Inputs may be any that keep to these rules, and one draw needn't show every extreme that they name: Supernode k owns the next widths[k] columns; the widths sum to 1536 and the widest is exactly 512.
All inputs are finite; a program needn't handle non-finite values.
Results may differ from a plain program's by a relative error of at most 0.001.
Values may be sent and summed in bfloat16 or wider, within the bound.
No kernel may reach another device: no remote copies, remote signals or barrier semaphores. Data moves between devices by JAX's collectives and lax.ppermute only.
A program may use at most 64 MiB of HBM per device.

v0:
```python
import functools

import jax
import jax.numpy as jnp
from jax import lax
from jax.experimental import pallas as pl
from jax.experimental.pallas import tpu as pltpu
from jax.sharding import PartitionSpec as P


SMEM = pl.BlockSpec(memory_space=pltpu.SMEM)


def column_onehot(widths, first, count, groups):
    ends = jnp.cumsum(widths, dtype=jnp.int32)
    columns = first + jnp.arange(count, dtype=jnp.int32)
    owner = jnp.sum((columns[:, None] >= ends[None, :]).astype(jnp.int32), axis=1)
    return (owner[:, None] == jnp.arange(groups, dtype=jnp.int32)[None, :]).astype(jnp.float32)


def plain_body(ainv, panel, structure, widths):
    rows_here, _, blk, cols_here, _, _ = ainv.shape
    groups = structure.shape[0]
    nprow = lax.axis_size("prow")
    npcol = lax.axis_size("pcol")
    row_id = lax.axis_index("prow")
    col_id = lax.axis_index("pcol")
    width_in = panel.shape[3]
    total = width_in * nprow
    width_out = total // npcol
    struct_float = structure.astype(jnp.float32)
    panel_struct = lax.dynamic_slice_in_dim(
        struct_float.reshape(groups, cols_here, npcol), col_id, 1, 2
    )[:, :, 0]
    onehot_in = column_onehot(widths, row_id * width_in, width_in, groups)
    keep_in = jnp.dot(panel_struct.T, onehot_in.T)
    masked = panel[:, 0] * keep_in[:, None, :].astype(jnp.bfloat16)
    amat = ainv.reshape(rows_here * blk, cols_here * blk)
    piece = lax.all_gather(masked, "prow", axis=2, tiled=True)
    partial_prod = jnp.dot(
        amat, piece.reshape(cols_here * blk, piece.shape[2]), preferred_element_type=jnp.float32
    )
    summed = lax.psum_scatter(partial_prod, "pcol", scatter_dimension=1, tiled=True)
    out_struct = lax.dynamic_slice_in_dim(
        struct_float.reshape(groups, rows_here, nprow), row_id, 1, 2
    )[:, :, 0]
    onehot_out = column_onehot(widths, col_id * width_out, width_out, groups)
    keep_out = jnp.dot(out_struct.T, onehot_out.T)
    result = -(summed.reshape(rows_here, blk, width_out) * keep_out[:, None, :])
    return result.astype(jnp.bfloat16).reshape(rows_here, 1, blk, width_out)


def ring_pos(row, n):
    return jnp.where(row % 2 == 0, row // 2, n - 1 - row // 2)


def ring_row(pos, n):
    return jnp.where(pos < n // 2, 2 * pos, 2 * (n - 1 - pos) + 1)


def owner_masks(widths_ref, first, rows, groups):
    cols = first + lax.broadcasted_iota(jnp.int32, (rows, 128), 0)
    masks, low = [], 0
    for k in range(groups):
        high = low + widths_ref[k]
        masks.append(((cols >= low) & (cols < high)).astype(jnp.float32))
        low = high
    return masks


def keep_of(masks, struct_ref, block):
    total = None
    for k, mask in enumerate(masks):
        term = mask * struct_ref[k, block].astype(jnp.float32)
        total = term if total is None else total + term
    return total


def multiply_kernel(offsets, n, npcol, width, struct_ref, widths_ref, *refs):
    count = len(offsets)
    panels, (own_ref, other_ref, send_ref, hold_ref, masked) = refs[: 2 * count], refs[2 * count :]
    depth, half, blk = panels[0].shape
    groups = struct_ref.shape[0]
    col = lax.axis_index("pcol")
    pos = ring_pos(lax.axis_index("prow"), n)

    @pl.when(pl.program_id(0) == 0)
    def _():
        for u, offset in enumerate(offsets):
            row = ring_row(lax.rem(pos + offset + n, n), n)
            masks = owner_masks(widths_ref, row * width + (col % 2) * half, half, groups)
            for q in range(2):
                part = col if q == 0 else col + 1 - 2 * (col % 2)
                for b in range(depth):
                    keep = keep_of(masks, struct_ref, b * npcol + part).astype(jnp.bfloat16)
                    for s in range(blk // 128):
                        at = pl.ds(s * 128, 128)
                        masked[q * depth + b, pl.ds(u * half, half), at] = (
                            panels[2 * u + q][b, :, at] * keep
                        )

    total = None
    for q, a_ref in enumerate((own_ref, other_ref)):
        for b in range(depth):
            term = lax.dot_general(
                masked[q * depth + b],
                a_ref[0, b],
                (((1,), (1,)), ((), ())),
                preferred_element_type=jnp.float32,
            )
            total = term if total is None else total + term
    first = (col // 2) == 0
    part = half // 2
    for u in range(count):
        low = total[u * half : u * half + part]
        high = total[u * half + part : (u + 1) * half]
        hold_ref[u] = jnp.where(first, low, high)
        send_ref[u] = jnp.where(first, high, low)


def multiply(offsets, n, npcol, width, structure, widths, panels, own, other):
    count = len(offsets)
    depth, half, blk = panels[0].shape
    rows = own.shape[0]
    shape = jax.ShapeDtypeStruct((count, half // 2, rows * blk), jnp.float32)
    whole = pl.BlockSpec((depth, half, blk), lambda a: (0, 0, 0))
    ablock = pl.BlockSpec((1, depth, blk, blk), lambda a: (a, 0, 0, 0))
    oblock = pl.BlockSpec((count, half // 2, blk), lambda a: (0, 0, a))
    flops = 2 * count * half * 2 * depth * blk * rows * blk
    return pl.pallas_call(
        functools.partial(multiply_kernel, offsets, n, npcol, width),
        grid=(rows,),
        in_specs=[SMEM, SMEM] + [whole] * (2 * count) + [ablock] * 2,
        out_specs=[oblock, oblock],
        out_shape=[shape, shape],
        scratch_shapes=[pltpu.VMEM((2 * depth, count * half, blk), jnp.bfloat16)],
        cost_estimate=pl.CostEstimate(
            flops=flops, bytes_accessed=4 * own.size + 4 * count * half * depth * blk, transcendentals=0
        ),
        compiler_params=pltpu.CompilerParams(vmem_limit_bytes=16 << 20),
    )(structure, widths, *panels, own, other)


def finish_kernel(offsets, n, width, struct_ref, widths_ref, hold_ref, got_ref, out_ref):
    _, part, height = hold_ref.shape
    groups = struct_ref.shape[0]
    me = lax.axis_index("prow")
    col = lax.axis_index("pcol")
    pos = ring_pos(me, n)
    blocks = struct_ref.shape[1] // n
    blk = height // blocks
    for u, offset in enumerate(offsets):
        row = ring_row(lax.rem(pos + offset + n, n), n)
        first = row * width + (col % 2) * 2 * part + (col // 2) * part
        masks = owner_masks(widths_ref, first, part, groups)
        for a in range(blocks):
            keep = keep_of(masks, struct_ref, a * n + me)
            for s in range(blk // 128):
                at = pl.ds(a * blk + s * 128, 128)
                value = -((hold_ref[u, :, at] + got_ref[u, :, at]) * keep)
                out_ref[u, :, at] = value.astype(jnp.bfloat16)


def finish(offsets, n, width, structure, widths, hold, got):
    whole = pl.BlockSpec(memory_space=pltpu.VMEM)
    return pl.pallas_call(
        functools.partial(finish_kernel, offsets, n, width),
        in_specs=[SMEM, SMEM, whole, whole],
        out_specs=whole,
        out_shape=jax.ShapeDtypeStruct(hold.shape, jnp.bfloat16),
        cost_estimate=pl.CostEstimate(flops=hold.size * 3, bytes_accessed=hold.size * 10, transcendentals=0),
        compiler_params=pltpu.CompilerParams(vmem_limit_bytes=4 << 20),
        name="finish",
    )(structure, widths, hold, got)


def pick_kernel(offsets, n, *refs):
    parts, outs, store = refs[: len(offsets)], refs[len(offsets) : -1], refs[-1]
    col = lax.axis_index("pcol")
    pos = ring_pos(lax.axis_index("prow"), n)
    for ref, here in zip(parts, offsets):
        for u, offset in enumerate(here):
            store[offset % n] = ref[u]
    for j, out in enumerate(outs):
        to = col ^ j
        for y in range(2):
            out[y] = store[lax.rem(ring_pos(2 * to + y, n) - pos + n, n)]


def pick(offsets, n, npcol, parts):
    whole = pl.BlockSpec(memory_space=pltpu.VMEM)
    _, part, height = parts[0].shape
    shape = jax.ShapeDtypeStruct((n // npcol, part, height), jnp.bfloat16)
    return pl.pallas_call(
        functools.partial(pick_kernel, offsets, n),
        in_specs=[whole] * len(parts),
        out_specs=[whole] * npcol,
        out_shape=[shape] * npcol,
        scratch_shapes=[pltpu.VMEM((n, part, height), jnp.bfloat16)],
        compiler_params=pltpu.CompilerParams(vmem_limit_bytes=6 << 20),
        name="pick",
    )(*parts)


def lay_kernel(width, *refs):
    parts, out_ref, store = refs[:-2], refs[-2], refs[-1]
    count, part, _ = parts[0].shape
    col = lax.axis_index("pcol")
    for j, ref in enumerate(parts):
        source = col ^ j
        start = (source % 2) * 2 * part + (source // 2) * part
        for y in range(count):
            at = pl.multiple_of(y * width + start, 16)
            store[pl.ds(at, part), :] = ref[y].astype(jnp.float32)
    blocks, blk, _ = out_ref.shape
    for a in range(blocks):
        out_ref[a] = store[:, a * blk : (a + 1) * blk].T.astype(jnp.bfloat16)


def lay(width, blocks, parts):
    whole = pl.BlockSpec(memory_space=pltpu.VMEM)
    count, _, height = parts[0].shape
    columns = count * width
    return pl.pallas_call(
        functools.partial(lay_kernel, width),
        in_specs=[whole] * len(parts),
        out_specs=whole,
        out_shape=jax.ShapeDtypeStruct((blocks, height // blocks, columns), jnp.bfloat16),
        scratch_shapes=[pltpu.VMEM((columns, height), jnp.float32)],
        compiler_params=pltpu.CompilerParams(vmem_limit_bytes=8 << 20),
        name="lay",
    )(*parts)


def ring_body(ainv, panel, structure, widths):
    n = lax.axis_size("prow")
    npcol = lax.axis_size("pcol")
    half_way = n // 2
    width = panel.shape[3]
    half = width // 2
    ring = list(range(0, n, 2)) + list(range(n - 1, 0, -2))
    up = [(ring[i], ring[(i + 1) % n]) for i in range(n)]
    down = [(ring[(i + 1) % n], ring[i]) for i in range(n)]
    side = [(c, c ^ 1) for c in range(npcol)]
    across = [(c, c ^ 2) for c in range(npcol)]
    core = lax.axis_index("pcol") % 2

    own = jnp.transpose(ainv, (0, 1, 3, 4, 2, 5))[:, 0, :, 0]
    cols = jnp.transpose(panel, (0, 1, 3, 2))[:, 0]
    mine = lax.dynamic_slice_in_dim(cols, core * half, half, 1)
    theirs = lax.dynamic_slice_in_dim(cols, (1 - core) * half, half, 1)
    partner = lax.ppermute(theirs, "pcol", side)
    other = lax.ppermute(own, "pcol", side)
    a_up, a_down, b_up, b_down = [mine], [mine], [partner], [partner]
    for _ in range(1, half_way):
        a_up.append(lax.ppermute(a_up[-1], "prow", up))
        a_down.append(lax.ppermute(a_down[-1], "prow", down))
        b_up.append(lax.ppermute(b_up[-1], "prow", up))
        b_down.append(lax.ppermute(b_down[-1], "prow", down))
    a_last = lax.ppermute(a_up[-1], "prow", up)
    b_last = lax.ppermute(b_down[-1], "prow", down)

    stages = [((0,), (mine, partner))]
    for s in range(1, half_way):
        stages.append(((-s, s), (a_up[s], b_up[s], a_down[s], b_down[s])))
    stages.append(((half_way,), (a_last, b_last)))

    done = []
    for offsets, panels in stages:
        send, hold = multiply(offsets, n, npcol, width, structure, widths, panels, own, other)
        got = lax.ppermute(send, "pcol", across)
        done.append(finish(offsets, n, width, structure, widths, hold, got))

    kept, *sends = pick([o for o, _ in stages], n, npcol, done)
    parts = [kept]
    for j, send in enumerate(sends, 1):
        parts.append(lax.ppermute(send, "pcol", [(c, c ^ j) for c in range(npcol)]))
    out = lay(width, own.shape[0], parts)
    return out[:, None]


def solution(mesh):
    in_specs = (P(None, "prow", None, None, "pcol", None), P(None, "pcol", None, "prow"), P(), P())
    out_specs = P(None, "prow", None, "pcol")
    n, npcol = mesh.shape["prow"], mesh.shape["pcol"]
    two_chips = npcol == 2 * 2 and n % 2 == 0 and n == 2 * npcol
    if not two_chips:
        return jax.shard_map(plain_body, mesh=mesh, in_specs=in_specs, out_specs=out_specs, check_vma=False)
    return jax.shard_map(
        ring_body, mesh=mesh, in_specs=in_specs, out_specs=out_specs, check_vma=False
    )
```

profile of v0, /device:TPU:0, one launch (start us, length us, event | category | flops | bytes accessed | tf_op | source)
XLA Modules:
  0.0 88.7 jit_solution(11726040178594438214)
XLA Ops:
  0.0 0.5 collective-permute-start.1
  0.5 1.1 %dynamic-slice_bitcast_fusion = (bf16[6,96,256]{2,1,0:T(8,128)(2,1)S(1)}, bf16[6,96,256]{2,1,0:T(8,128)(2,1)S(1)}) fusion(bf16[6,1,256,192]{2,3,0,1:T(8,128)(2,1)} %bitcast.23, s32[]{:T(128)S(6)} %select_n.15, s32[]{:T(128)S(6)} %select_n.14), kind=kLoop, calls=%fused_computation | loop fusion | bytes 1179656 | tf_op jit(solution)/shard_map/dynamic_slice | solution.py:251
  1.6 0.1 collective-permute-start
  1.7 3.1 %collective-permute-start.3 = (bf16[6,96,256]{2,1,0:T(8,128)(2,1)S(1)}, bf16[6,96,256]{2,1,0:T(8,128)(2,1)S(1)}, u32[]{:S(2)}, u32[]{:S(2)}) collective-permute-start(bf16[6,96,256]{2,1,0:T(8,128)(2,1)S(1)} %get-tuple-element.34.refs_0_), channel_id=1, source_target_pairs={{0,8},{8,16},{16,24},{24,28},{28,20},{20,12},{12,4},{4,0},{1,9},{9... | collective-permute-start | bytes 884744 | tf_op jit(solution)/shard_map/ppermute | solution.py:256
  4.7 0.6 collective-permute-done.refs_1_
  5.3 2.9 %collective-permute-start.6 = (bf16[6,96,256]{2,1,0:T(8,128)(2,1)S(1)}, bf16[6,96,256]{2,1,0:T(8,128)(2,1)S(1)}, u32[]{:S(2)}, u32[]{:S(2)}) collective-permute-start(bf16[6,96,256]{2,1,0:T(8,128)(2,1)S(1)} %collective-permute-done.refs_1_), channel_id=1, source_target_pairs={{8,0},{16,8},{24,16},{28,24},{20,28},{12,20},{4,12},{0,4},{9,1},{1... | collective-permute-start | bytes 884744 | tf_op jit(solution)/shard_map/ppermute | solution.py:259
  8.2 1.6 %collective-permute-start.5 = (bf16[6,96,256]{2,1,0:T(8,128)(2,1)S(1)}, bf16[6,96,256]{2,1,0:T(8,128)(2,1)S(1)}, u32[]{:S(2)}, u32[]{:S(2)}) collective-permute-start(bf16[6,96,256]{2,1,0:T(8,128)(2,1)S(1)} %get-tuple-element.34.refs_0_), channel_id=1, source_target_pairs={{8,0},{16,8},{24,16},{28,24},{20,28},{12,20},{4,12},{0,4},{9,1},{1... | collective-permute-start | bytes 884744 | tf_op jit(solution)/shard_map/ppermute | solution.py:257
  9.7 0.4 collective-permute-start.4
  10.2 1.9 %collective-permute-done.3.refs_0_ = bf16[6,96,256]{2,1,0:T(8,128)(2,1)S(1)} collective-permute-done((bf16[6,96,256]{2,1,0:T(8,128)(2,1)S(1)}, bf16[6,96,256]{2,1,0:T(8,128)(2,1)S(1)}, u32[]{:S(2)}, u32[]{:S(2)}) %collective-permute-start.3) | collective-permute-done | bytes 294944 | tf_op jit(solution)/shard_map/ppermute | solution.py:256
  12.1 2.5 %collective-permute-start.8 = (bf16[6,96,256]{2,1,0:T(8,128)(2,1)S(1)}, bf16[6,96,256]{2,1,0:T(8,128)(2,1)S(1)}, u32[]{:S(2)}, u32[]{:S(2)}) collective-permute-start(bf16[6,96,256]{2,1,0:T(8,128)(2,1)S(1)} %collective-permute-done.3.refs_0_), channel_id=1, source_target_pairs={{0,8},{8,16},{16,24},{24,28},{28,20},{20,12},{12,4},{4,0},{1,9},{9... | collective-permute-start | bytes 884744 | tf_op jit(solution)/shard_map/ppermute | solution.py:256
  14.6 1.5 %collective-permute-done.6.refs_3_ = bf16[6,96,256]{2,1,0:T(8,128)(2,1)S(1)} collective-permute-done((bf16[6,96,256]{2,1,0:T(8,128)(2,1)S(1)}, bf16[6,96,256]{2,1,0:T(8,128)(2,1)S(1)}, u32[]{:S(2)}, u32[]{:S(2)}) %collective-permute-start.6) | collective-permute-done | bytes 294944 | tf_op jit(solution)/shard_map/ppermute | solution.py:259
  16.1 2.0 %collective-permute-start.11 = (bf16[6,96,256]{2,1,0:T(8,128)(2,1)S(1)}, bf16[6,96,256]{2,1,0:T(8,128)(2,1)S(1)}, u32[]{:S(2)}, u32[]{:S(2)}) collective-permute-start(bf16[6,96,256]{2,1,0:T(8,128)(2,1)S(1)} %collective-permute-done.6.refs_3_), channel_id=1, source_target_pairs={{8,0},{16,8},{24,16},{28,24},{20,28},{12,20},{4,12},{0,4},{9,1},{1... | collective-permute-start | bytes 884744 | tf_op jit(solution)/shard_map/ppermute | solution.py:259
  18.0 4.4 %collective-permute-done.5.refs_2_ = bf16[6,96,256]{2,1,0:T(8,128)(2,1)S(1)} collective-permute-done((bf16[6,96,256]{2,1,0:T(8,128)(2,1)S(1)}, bf16[6,96,256]{2,1,0:T(8,128)(2,1)S(1)}, u32[]{:S(2)}, u32[]{:S(2)}) %collective-permute-start.5) | collective-permute-done | bytes 294944 | tf_op jit(solution)/shard_map/ppermute | solution.py:257
  22.4 2.0 %collective-permute-start.10 = (bf16[6,96,256]{2,1,0:T(8,128)(2,1)S(1)}, bf16[6,96,256]{2,1,0:T(8,128)(2,1)S(1)}, u32[]{:S(2)}, u32[]{:S(2)}) collective-permute-start(bf16[6,96,256]{2,1,0:T(8,128)(2,1)S(1)} %collective-permute-done.5.refs_2_), channel_id=1, source_target_pairs={{8,0},{16,8},{24,16},{28,24},{20,28},{12,20},{4,12},{0,4},{9,1},{1... | collective-permute-start | bytes 884744 | tf_op jit(solution)/shard_map/ppermute | solution.py:257
  24.4 0.0 collective-permute-done.4.refs_1_
  24.4 0.1 collective-permute-start.9
  24.4 0.1 collective-permute-done.8.refs_0_
  24.6 2.4 %collective-permute-start.13 = (bf16[6,96,256]{2,1,0:T(8,128)(2,1)S(1)}, bf16[6,96,256]{2,1,0:T(8,128)(2,1)S(1)}, u32[]{:S(2)}, u32[]{:S(2)}) collective-permute-start(bf16[6,96,256]{2,1,0:T(8,128)(2,1)S(1)} %collective-permute-done.8.refs_0_), channel_id=1, source_target_pairs={{0,8},{8,16},{16,24},{24,28},{28,20},{20,12},{12,4},{4,0},{1,9},{9... | collective-permute-start | bytes 884744 | tf_op jit(solution)/shard_map/ppermute | solution.py:256
  26.9 1.8 %collective-permute-done.11.refs_3_ = bf16[6,96,256]{2,1,0:T(8,128)(2,1)S(1)} collective-permute-done((bf16[6,96,256]{2,1,0:T(8,128)(2,1)S(1)}, bf16[6,96,256]{2,1,0:T(8,128)(2,1)S(1)}, u32[]{:S(2)}, u32[]{:S(2)}) %collective-permute-start.11) | collective-permute-done | bytes 294944 | tf_op jit(solution)/shard_map/ppermute | solution.py:259
  28.7 2.0 %collective-permute-start.16 = (bf16[6,96,256]{2,1,0:T(8,128)(2,1)S(1)}, bf16[6,96,256]{2,1,0:T(8,128)(2,1)S(1)}, u32[]{:S(2)}, u32[]{:S(2)}) collective-permute-start(bf16[6,96,256]{2,1,0:T(8,128)(2,1)S(1)} %collective-permute-done.11.refs_3_), channel_id=1, source_target_pairs={{8,0},{16,8},{24,16},{28,24},{20,28},{12,20},{4,12},{0,4},{9,1},{1... | collective-permute-start | bytes 884744 | tf_op jit(solution)/shard_map/ppermute | solution.py:259
  30.7 4.4 %collective-permute-done.10.refs_2_ = bf16[6,96,256]{2,1,0:T(8,128)(2,1)S(1)} collective-permute-done((bf16[6,96,256]{2,1,0:T(8,128)(2,1)S(1)}, bf16[6,96,256]{2,1,0:T(8,128)(2,1)S(1)}, u32[]{:S(2)}, u32[]{:S(2)}) %collective-permute-start.10) | collective-permute-done | bytes 294944 | tf_op jit(solution)/shard_map/ppermute | solution.py:257
  35.0 2.0 %collective-permute-start.15 = (bf16[6,96,256]{2,1,0:T(8,128)(2,1)S(1)}, bf16[6,96,256]{2,1,0:T(8,128)(2,1)S(1)}, u32[]{:S(2)}, u32[]{:S(2)}) collective-permute-start(bf16[6,96,256]{2,1,0:T(8,128)(2,1)S(1)} %collective-permute-done.10.refs_2_), channel_id=1, source_target_pairs={{8,0},{16,8},{24,16},{28,24},{20,28},{12,20},{4,12},{0,4},{9,1},{1... | collective-permute-start | bytes 884744 | tf_op jit(solution)/shard_map/ppermute | solution.py:257
  37.0 0.0 collective-permute-done.9.refs_1_
  37.0 0.1 collective-permute-start.14
  37.1 0.7 collective-permute-done.13.refs_0_
  37.8 1.8 %collective-permute-start.18 = (bf16[6,96,256]{2,1,0:T(8,128)(2,1)S(1)}, bf16[6,96,256]{2,1,0:T(8,128)(2,1)S(1)}, u32[]{:S(2)}, u32[]{:S(2)}) collective-permute-start(bf16[6,96,256]{2,1,0:T(8,128)(2,1)S(1)} %collective-permute-done.13.refs_0_), channel_id=1, source_target_pairs={{0,8},{8,16},{16,24},{24,28},{28,20},{20,12},{12,4},{4,0},{1,9},{9... | collective-permute-start | bytes 884744 | tf_op jit(solution)/shard_map/ppermute | solution.py:260
  39.6 1.8 %collective-permute-done.16.refs_3_ = bf16[6,96,256]{2,1,0:T(8,128)(2,1)S(1)} collective-permute-done((bf16[6,96,256]{2,1,0:T(8,128)(2,1)S(1)}, bf16[6,96,256]{2,1,0:T(8,128)(2,1)S(1)}, u32[]{:S(2)}, u32[]{:S(2)}) %collective-permute-start.16) | collective-permute-done | bytes 294944 | tf_op jit(solution)/shard_map/ppermute | solution.py:259
  41.4 2.0 %collective-permute-start.19 = (bf16[6,96,256]{2,1,0:T(8,128)(2,1)S(1)}, bf16[6,96,256]{2,1,0:T(8,128)(2,1)S(1)}, u32[]{:S(2)}, u32[]{:S(2)}) collective-permute-start(bf16[6,96,256]{2,1,0:T(8,128)(2,1)S(1)} %collective-permute-done.16.refs_3_), channel_id=1, source_target_pairs={{8,0},{16,8},{24,16},{28,24},{20,28},{12,20},{4,12},{0,4},{9,1},{1... | collective-permute-start | bytes 884744 | tf_op jit(solution)/shard_map/ppermute | solution.py:261
  43.3 0.0 collective-permute-done.1.refs_3_.refs_5_
  43.3 1.7 %copy-done = bf16[3,1,256,6,1,256]{5,2,4,3,1,0:T(8,128)(2,1)S(1)} copy-done((bf16[3,1,256,6,1,256]{5,2,4,3,1,0:T(8,128)(2,1)S(1)}, bf16[3,1,256,6,1,256]{5,2,4,3,1,0:T(8,128)(2,1)}, u32[]{:S(2)}) %copy-start) | copy-done | bytes 2359320
  45.0 0.7 copy-done.2
  45.7 0.7 copy-done.3
  46.3 3.3 %shard_map.47 = (f32[2,48,768]{2,1,0:T(8,128)S(1)}, f32[2,48,768]{2,1,0:T(8,128)S(1)}) custom-call(s32[4,24]{1,0:T(4,128)S(1)} %copy-done.2, s32[4]{0:T(128)S(1)} %copy-done.3, bf16[6,96,256]{2,1,0:T(8,128)(2,1)S(1)} %collective-permute-done.3.refs_0_, bf16[6,96,256]{2,1,0:T(8,128)(2,1)S(1)} %collective-permute-done.4.refs_1_, ...), custom_call_target="tpu_custom_call" | custom-call | flops 905969664 | bytes 5898240 | tf_op jit(solution)/shard_map/pallas_call | solution.py:130
  49.6 1.6 %collective-permute-start.7 = (f32[2,48,768]{2,1,0:T(8,128)S(1)}, f32[2,48,768]{2,1,0:T(8,128)S(1)}, u32[]{:S(2)}, u32[]{:S(2)}) collective-permute-start(f32[2,48,768]{2,1,0:T(8,128)S(1)} %get-tuple-element.22), channel_id=1, source_target_pairs={{0,2},{1,3},{2,0},{3,1},{4,6},{5,7},{6,4},{7,5},{8,10},{9,11},{10,... | collective-permute-start | bytes 884744 | tf_op jit(solution)/shard_map/ppermute | solution.py:271
  51.2 3.3 %shard_map.48 = (f32[2,48,768]{2,1,0:T(8,128)S(1)}, f32[2,48,768]{2,1,0:T(8,128)S(1)}) custom-call(s32[4,24]{1,0:T(4,128)S(1)} %copy-done.2, s32[4]{0:T(128)S(1)} %copy-done.3, bf16[6,96,256]{2,1,0:T(8,128)(2,1)S(1)} %collective-permute-done.8.refs_0_, bf16[6,96,256]{2,1,0:T(8,128)(2,1)S(1)} %collective-permute-done.9.refs_1_, ...), custom_call_target="tpu_custom_call" | custom-call | flops 905969664 | bytes 5898240 | tf_op jit(solution)/shard_map/pallas_call | solution.py:130
  54.5 0.0 collective-permute-done.15.refs_2_
  54.5 0.0 copy-start.1
  54.5 0.6 collective-permute-start.12
  55.1 0.0 collective-permute-done.14.refs_1_
  55.1 3.3 %shard_map.49 = (f32[2,48,768]{2,1,0:T(8,128)S(1)}, f32[2,48,768]{2,1,0:T(8,128)S(1)}) custom-call(s32[4,24]{1,0:T(4,128)S(1)} %copy-done.2, s32[4]{0:T(128)S(1)} %copy-done.3, bf16[6,96,256]{2,1,0:T(8,128)(2,1)S(1)} %collective-permute-done.13.refs_0_, bf16[6,96,256]{2,1,0:T(8,128)(2,1)S(1)} %collective-permute-done.14.refs_1_, ...), custom_call_target="tpu_custom_call" | custom-call | flops 905969664 | bytes 5898240 | tf_op jit(solution)/shard_map/pallas_call | solution.py:130
  58.4 1.6 %collective-permute-start.17 = (f32[2,48,768]{2,1,0:T(8,128)S(1)}, f32[2,48,768]{2,1,0:T(8,128)S(1)}, u32[]{:S(2)}, u32[]{:S(2)}) collective-permute-start(f32[2,48,768]{2,1,0:T(8,128)S(1)} %get-tuple-element.26), channel_id=1, source_target_pairs={{0,2},{1,3},{2,0},{3,1},{4,6},{5,7},{6,4},{7,5},{8,10},{9,11},{10,... | collective-permute-start | bytes 884744 | tf_op jit(solution)/shard_map/ppermute | solution.py:271
  60.0 2.8 %shard_map.46 = (f32[1,48,768]{2,1,0:T(8,128)S(1)}, f32[1,48,768]{2,1,0:T(8,128)S(1)}) custom-call(s32[4,24]{1,0:T(4,128)S(1)} %copy-done.2, s32[4]{0:T(128)S(1)} %copy-done.3, bf16[6,96,256]{2,1,0:T(8,128)(2,1)S(1)} %get-tuple-element.34.refs_0_, bf16[6,96,256]{2,1,0:T(8,128)(2,1)S(1)} %collective-permute-done.refs_1_, ...), custom_call_target="tpu_custom_call" | custom-call | flops 452984832 | bytes 5308416 | tf_op jit(solution)/shard_map/pallas_call | solution.py:130
  62.8 0.0 collective-permute-done.18.refs_0_
  62.8 0.6 collective-permute-start.2
  63.4 0.0 collective-permute-done.19.refs_1_
  63.4 2.8 %shard_map.50 = (f32[1,48,768]{2,1,0:T(8,128)S(1)}, f32[1,48,768]{2,1,0:T(8,128)S(1)}) custom-call(s32[4,24]{1,0:T(4,128)S(1)} %copy-done.2, s32[4]{0:T(128)S(1)} %copy-done.3, bf16[6,96,256]{2,1,0:T(8,128)(2,1)S(1)} %collective-permute-done.18.refs_0_, bf16[6,96,256]{2,1,0:T(8,128)(2,1)S(1)} %collective-permute-done.19.refs_1_, ...), custom_call_target="tpu_custom_call" | custom-call | flops 452984832 | bytes 5308416 | tf_op jit(solution)/shard_map/pallas_call | solution.py:130
  66.2 1.6 %collective-permute-start.20 = (f32[1,48,768]{2,1,0:T(8,128)S(1)}, f32[1,48,768]{2,1,0:T(8,128)S(1)}, u32[]{:S(2)}, u32[]{:S(2)}) collective-permute-start(f32[1,48,768]{2,1,0:T(8,128)S(1)} %get-tuple-element.28), channel_id=1, source_target_pairs={{0,2},{1,3},{2,0},{3,1},{4,6},{5,7},{6,4},{7,5},{8,10},{9,11},{10,... | collective-permute-start | bytes 442376 | tf_op jit(solution)/shard_map/ppermute | solution.py:271
  67.8 6.4 %collective-permute-done.2.got_ref = f32[1,48,768]{2,1,0:T(8,128)S(1)} collective-permute-done((f32[1,48,768]{2,1,0:T(8,128)S(1)}, f32[1,48,768]{2,1,0:T(8,128)S(1)}, u32[]{:S(2)}, u32[]{:S(2)}) %collective-permute-start.2) | collective-permute-done | bytes 147488 | tf_op jit(solution)/shard_map/ppermute | solution.py:271
  74.2 0.6 finish.5.refs_0_
  74.8 0.9 %collective-permute-done.20.got_ref = f32[1,48,768]{2,1,0:T(8,128)S(1)} collective-permute-done((f32[1,48,768]{2,1,0:T(8,128)S(1)}, f32[1,48,768]{2,1,0:T(8,128)S(1)}, u32[]{:S(2)}, u32[]{:S(2)}) %collective-permute-start.20) | collective-permute-done | bytes 147488 | tf_op jit(solution)/shard_map/ppermute | solution.py:271
  75.7 0.6 finish.9.refs_4_
  76.4 0.0 collective-permute-done.7.got_ref
  76.4 0.7 finish.6.refs_1_
  77.1 0.0 collective-permute-done.12.got_ref
  77.1 0.7 finish.7.refs_2_
  77.8 0.0 collective-permute-done.17.got_ref
  77.8 0.7 finish.8.refs_3_
  78.5 0.1 pick.1
  78.6 0.1 collective-permute-start.21
  78.7 1.6 %collective-permute-start.22 = (bf16[2,48,768]{2,1,0:T(8,128)(2,1)S(1)}, bf16[2,48,768]{2,1,0:T(8,128)(2,1)S(1)}, u32[]{:S(2)}, u32[]{:S(2)}) collective-permute-start(bf16[2,48,768]{2,1,0:T(8,128)(2,1)S(1)} %get-tuple-element.31), channel_id=1, source_target_pairs={{0,2},{1,3},{2,0},{3,1},{4,6},{5,7},{6,4},{7,5},{8,10},{9,11},{10,... | collective-permute-start | bytes 442376 | tf_op jit(solution)/shard_map/ppermute | solution.py:277
  80.3 0.3 collective-permute-start.23
  80.6 4.9 %collective-permute-done.22.refs_2_ = bf16[2,48,768]{2,1,0:T(8,128)(2,1)S(1)} collective-permute-done((bf16[2,48,768]{2,1,0:T(8,128)(2,1)S(1)}, bf16[2,48,768]{2,1,0:T(8,128)(2,1)S(1)}, u32[]{:S(2)}, u32[]{:S(2)}) %collective-permute-start.22) | collective-permute-done | bytes 147488 | tf_op jit(solution)/shard_map/ppermute | solution.py:277
  85.5 2.1 %collective-permute-done.23.refs_3_ = bf16[2,48,768]{2,1,0:T(8,128)(2,1)S(1)} collective-permute-done((bf16[2,48,768]{2,1,0:T(8,128)(2,1)S(1)}, bf16[2,48,768]{2,1,0:T(8,128)(2,1)S(1)}, u32[]{:S(2)}, u32[]{:S(2)}) %collective-permute-start.23) | collective-permute-done | bytes 147488 | tf_op jit(solution)/shard_map/ppermute | solution.py:277
  87.6 1.1 %lay.1 = bf16[3,256,384]{2,1,0:T(8,128)(2,1)} custom-call(bf16[2,48,768]{2,1,0:T(8,128)(2,1)S(1)} %get-tuple-element.29.refs_0_, bf16[2,48,768]{2,1,0:T(8,128)(2,1)S(1)} %collective-permute-done.21.refs_1_, bf16[2,48,768]{2,1,0:T(8,128)(2,1)S(1)} %collective-permute-done.22.refs_2_, bf16[2,48,768]{2,1,0:T(8,128)(2,1)S(1)} %collective-permute-done.23.refs_3_), custom_call_target="tpu_custom_call" | custom-call | tf_op jit(solution)/shard_map/lay/pallas_call | solution.py:224
  (5 shorter events, 0.0 us)
Async XLA Ops:
  0.0 43.3 %collective-permute-start.1 = (bf16[3,6,256,256]{3,2,1,0:T(8,128)(2,1)}, bf16[3,6,256,256]{3,2,1,0:T(8,128)(2,1)S(1)}, u32[]{:S(2)}, u32[]{:S(2)}) collective-permute-start(bf16[3,6,256,256]{3,2,1,0:T(8,128)(2,1)} %bitcast.17), channel_id=1, source_target_pairs={{0,1},{1,0},{2,3},{3,2},{4,5},{5,4},{6,7},{7,6},{8,9},{9,8},{10,11... | collective-permute-start | bytes 7077896 | tf_op jit(solution)/shard_map/ppermute | solution.py:253
  1.6 3.7 %collective-permute-start = (bf16[6,96,256]{2,1,0:T(8,128)(2,1)S(1)}, bf16[6,96,256]{2,1,0:T(8,128)(2,1)S(1)}, u32[]{:S(2)}, u32[]{:S(2)}) collective-permute-start(bf16[6,96,256]{2,1,0:T(8,128)(2,1)S(1)} %get-tuple-element.33), channel_id=1, source_target_pairs={{0,1},{1,0},{2,3},{3,2},{4,5},{5,4},{6,7},{7,6},{8,9},{9,8},{10,11... | collective-permute-start | bytes 884744 | tf_op jit(solution)/shard_map/ppermute | solution.py:252
  1.7 10.4 %collective-permute-start.3 = (bf16[6,96,256]{2,1,0:T(8,128)(2,1)S(1)}, bf16[6,96,256]{2,1,0:T(8,128)(2,1)S(1)}, u32[]{:S(2)}, u32[]{:S(2)}) collective-permute-start(bf16[6,96,256]{2,1,0:T(8,128)(2,1)S(1)} %get-tuple-element.34.refs_0_), channel_id=1, source_target_pairs={{0,8},{8,16},{16,24},{24,28},{28,20},{20,12},{12,4},{4,0},{1,9},{9... | collective-permute-start | bytes 884744 | tf_op jit(solution)/shard_map/ppermute | solution.py:256
  5.3 10.8 %collective-permute-start.6 = (bf16[6,96,256]{2,1,0:T(8,128)(2,1)S(1)}, bf16[6,96,256]{2,1,0:T(8,128)(2,1)S(1)}, u32[]{:S(2)}, u32[]{:S(2)}) collective-permute-start(bf16[6,96,256]{2,1,0:T(8,128)(2,1)S(1)} %collective-permute-done.refs_1_), channel_id=1, source_target_pairs={{8,0},{16,8},{24,16},{28,24},{20,28},{12,20},{4,12},{0,4},{9,1},{1... | collective-permute-start | bytes 884744 | tf_op jit(solution)/shard_map/ppermute | solution.py:259
  8.2 14.2 %collective-permute-start.5 = (bf16[6,96,256]{2,1,0:T(8,128)(2,1)S(1)}, bf16[6,96,256]{2,1,0:T(8,128)(2,1)S(1)}, u32[]{:S(2)}, u32[]{:S(2)}) collective-permute-start(bf16[6,96,256]{2,1,0:T(8,128)(2,1)S(1)} %get-tuple-element.34.refs_0_), channel_id=1, source_target_pairs={{8,0},{16,8},{24,16},{28,24},{20,28},{12,20},{4,12},{0,4},{9,1},{1... | collective-permute-start | bytes 884744 | tf_op jit(solution)/shard_map/ppermute | solution.py:257
  9.7 14.6 %collective-permute-start.4 = (bf16[6,96,256]{2,1,0:T(8,128)(2,1)S(1)}, bf16[6,96,256]{2,1,0:T(8,128)(2,1)S(1)}, u32[]{:S(2)}, u32[]{:S(2)}) collective-permute-start(bf16[6,96,256]{2,1,0:T(8,128)(2,1)S(1)} %collective-permute-done.refs_1_), channel_id=1, source_target_pairs={{0,8},{8,16},{16,24},{24,28},{28,20},{20,12},{12,4},{4,0},{1,9},{9... | collective-permute-start | bytes 884744 | tf_op jit(solution)/shard_map/ppermute | solution.py:258
  12.1 12.4 %collective-permute-start.8 = (bf16[6,96,256]{2,1,0:T(8,128)(2,1)S(1)}, bf16[6,96,256]{2,1,0:T(8,128)(2,1)S(1)}, u32[]{:S(2)}, u32[]{:S(2)}) collective-permute-start(bf16[6,96,256]{2,1,0:T(8,128)(2,1)S(1)} %collective-permute-done.3.refs_0_), channel_id=1, source_target_pairs={{0,8},{8,16},{16,24},{24,28},{28,20},{20,12},{12,4},{4,0},{1,9},{9... | collective-permute-start | bytes 884744 | tf_op jit(solution)/shard_map/ppermute | solution.py:256
  16.1 12.6 %collective-permute-start.11 = (bf16[6,96,256]{2,1,0:T(8,128)(2,1)S(1)}, bf16[6,96,256]{2,1,0:T(8,128)(2,1)S(1)}, u32[]{:S(2)}, u32[]{:S(2)}) collective-permute-start(bf16[6,96,256]{2,1,0:T(8,128)(2,1)S(1)} %collective-permute-done.6.refs_3_), channel_id=1, source_target_pairs={{8,0},{16,8},{24,16},{28,24},{20,28},{12,20},{4,12},{0,4},{9,1},{1... | collective-permute-start | bytes 884744 | tf_op jit(solution)/shard_map/ppermute | solution.py:259
  22.4 12.6 %collective-permute-start.10 = (bf16[6,96,256]{2,1,0:T(8,128)(2,1)S(1)}, bf16[6,96,256]{2,1,0:T(8,128)(2,1)S(1)}, u32[]{:S(2)}, u32[]{:S(2)}) collective-permute-start(bf16[6,96,256]{2,1,0:T(8,128)(2,1)S(1)} %collective-permute-done.5.refs_2_), channel_id=1, source_target_pairs={{8,0},{16,8},{24,16},{28,24},{20,28},{12,20},{4,12},{0,4},{9,1},{1... | collective-permute-start | bytes 884744 | tf_op jit(solution)/shard_map/ppermute | solution.py:257
  24.4 12.6 %collective-permute-start.9 = (bf16[6,96,256]{2,1,0:T(8,128)(2,1)S(1)}, bf16[6,96,256]{2,1,0:T(8,128)(2,1)S(1)}, u32[]{:S(2)}, u32[]{:S(2)}) collective-permute-start(bf16[6,96,256]{2,1,0:T(8,128)(2,1)S(1)} %collective-permute-done.4.refs_1_), channel_id=1, source_target_pairs={{0,8},{8,16},{16,24},{24,28},{28,20},{20,12},{12,4},{4,0},{1,9},{9... | collective-permute-start | bytes 884744 | tf_op jit(solution)/shard_map/ppermute | solution.py:258
  24.6 13.2 %collective-permute-start.13 = (bf16[6,96,256]{2,1,0:T(8,128)(2,1)S(1)}, bf16[6,96,256]{2,1,0:T(8,128)(2,1)S(1)}, u32[]{:S(2)}, u32[]{:S(2)}) collective-permute-start(bf16[6,96,256]{2,1,0:T(8,128)(2,1)S(1)} %collective-permute-done.8.refs_0_), channel_id=1, source_target_pairs={{0,8},{8,16},{16,24},{24,28},{28,20},{20,12},{12,4},{4,0},{1,9},{9... | collective-permute-start | bytes 884744 | tf_op jit(solution)/shard_map/ppermute | solution.py:256
  28.7 12.6 %collective-permute-start.16 = (bf16[6,96,256]{2,1,0:T(8,128)(2,1)S(1)}, bf16[6,96,256]{2,1,0:T(8,128)(2,1)S(1)}, u32[]{:S(2)}, u32[]{:S(2)}) collective-permute-start(bf16[6,96,256]{2,1,0:T(8,128)(2,1)S(1)} %collective-permute-done.11.refs_3_), channel_id=1, source_target_pairs={{8,0},{16,8},{24,16},{28,24},{20,28},{12,20},{4,12},{0,4},{9,1},{1... | collective-permute-start | bytes 884744 | tf_op jit(solution)/shard_map/ppermute | solution.py:259
  35.0 19.4 %collective-permute-start.15 = (bf16[6,96,256]{2,1,0:T(8,128)(2,1)S(1)}, bf16[6,96,256]{2,1,0:T(8,128)(2,1)S(1)}, u32[]{:S(2)}, u32[]{:S(2)}) collective-permute-start(bf16[6,96,256]{2,1,0:T(8,128)(2,1)S(1)} %collective-permute-done.10.refs_2_), channel_id=1, source_target_pairs={{8,0},{16,8},{24,16},{28,24},{20,28},{12,20},{4,12},{0,4},{9,1},{1... | collective-permute-start | bytes 884744 | tf_op jit(solution)/shard_map/ppermute | solution.py:257
  37.0 18.1 %collective-permute-start.14 = (bf16[6,96,256]{2,1,0:T(8,128)(2,1)S(1)}, bf16[6,96,256]{2,1,0:T(8,128)(2,1)S(1)}, u32[]{:S(2)}, u32[]{:S(2)}) collective-permute-start(bf16[6,96,256]{2,1,0:T(8,128)(2,1)S(1)} %collective-permute-done.9.refs_1_), channel_id=1, source_target_pairs={{0,8},{8,16},{16,24},{24,28},{28,20},{20,12},{12,4},{4,0},{1,9},{9... | collective-permute-start | bytes 884744 | tf_op jit(solution)/shard_map/ppermute | solution.py:258
  37.8 25.0 %collective-permute-start.18 = (bf16[6,96,256]{2,1,0:T(8,128)(2,1)S(1)}, bf16[6,96,256]{2,1,0:T(8,128)(2,1)S(1)}, u32[]{:S(2)}, u32[]{:S(2)}) collective-permute-start(bf16[6,96,256]{2,1,0:T(8,128)(2,1)S(1)} %collective-permute-done.13.refs_0_), channel_id=1, source_target_pairs={{0,8},{8,16},{16,24},{24,28},{28,20},{20,12},{12,4},{4,0},{1,9},{9... | collective-permute-start | bytes 884744 | tf_op jit(solution)/shard_map/ppermute | solution.py:260
  41.4 22.0 %collective-permute-start.19 = (bf16[6,96,256]{2,1,0:T(8,128)(2,1)S(1)}, bf16[6,96,256]{2,1,0:T(8,128)(2,1)S(1)}, u32[]{:S(2)}, u32[]{:S(2)}) collective-permute-start(bf16[6,96,256]{2,1,0:T(8,128)(2,1)S(1)} %collective-permute-done.16.refs_3_), channel_id=1, source_target_pairs={{8,0},{16,8},{24,16},{28,24},{20,28},{12,20},{4,12},{0,4},{9,1},{1... | collective-permute-start | bytes 884744 | tf_op jit(solution)/shard_map/ppermute | solution.py:261
  43.3 1.7 %copy-start = (bf16[3,1,256,6,1,256]{5,2,4,3,1,0:T(8,128)(2,1)S(1)}, bf16[3,1,256,6,1,256]{5,2,4,3,1,0:T(8,128)(2,1)}, u32[]{:S(2)}) copy-start(bf16[3,1,256,6,1,256]{5,2,4,3,1,0:T(8,128)(2,1)} %param.4) | copy-start | bytes 7077892
  45.0 0.7 copy-start.2
  45.7 0.7 copy-start.3
  49.6 26.8 %collective-permute-start.7 = (f32[2,48,768]{2,1,0:T(8,128)S(1)}, f32[2,48,768]{2,1,0:T(8,128)S(1)}, u32[]{:S(2)}, u32[]{:S(2)}) collective-permute-start(f32[2,48,768]{2,1,0:T(8,128)S(1)} %get-tuple-element.22), channel_id=1, source_target_pairs={{0,2},{1,3},{2,0},{3,1},{4,6},{5,7},{6,4},{7,5},{8,10},{9,11},{10,... | collective-permute-start | bytes 884744 | tf_op jit(solution)/shard_map/ppermute | solution.py:271
  54.5 5.5 %copy-start.1 = (bf16[3,1,256,6,1,256]{5,2,4,3,1,0:T(8,128)(2,1)S(1)}, bf16[3,1,256,6,1,256]{5,2,4,3,1,0:T(8,128)(2,1)}, u32[]{:S(2)}) copy-start(bf16[3,1,256,6,1,256]{5,2,4,3,1,0:T(8,128)(2,1)} %param.4) | copy-start | bytes 7077892
  54.5 22.6 %collective-permute-start.12 = (f32[2,48,768]{2,1,0:T(8,128)S(1)}, f32[2,48,768]{2,1,0:T(8,128)S(1)}, u32[]{:S(2)}, u32[]{:S(2)}) collective-permute-start(f32[2,48,768]{2,1,0:T(8,128)S(1)} %get-tuple-element.24), channel_id=1, source_target_pairs={{0,2},{1,3},{2,0},{3,1},{4,6},{5,7},{6,4},{7,5},{8,10},{9,11},{10,... | collective-permute-start | bytes 884744 | tf_op jit(solution)/shard_map/ppermute | solution.py:271
  58.4 19.4 %collective-permute-start.17 = (f32[2,48,768]{2,1,0:T(8,128)S(1)}, f32[2,48,768]{2,1,0:T(8,128)S(1)}, u32[]{:S(2)}, u32[]{:S(2)}) collective-permute-start(f32[2,48,768]{2,1,0:T(8,128)S(1)} %get-tuple-element.26), channel_id=1, source_target_pairs={{0,2},{1,3},{2,0},{3,1},{4,6},{5,7},{6,4},{7,5},{8,10},{9,11},{10,... | collective-permute-start | bytes 884744 | tf_op jit(solution)/shard_map/ppermute | solution.py:271
  62.8 11.4 %collective-permute-start.2 = (f32[1,48,768]{2,1,0:T(8,128)S(1)}, f32[1,48,768]{2,1,0:T(8,128)S(1)}, u32[]{:S(2)}, u32[]{:S(2)}) collective-permute-start(f32[1,48,768]{2,1,0:T(8,128)S(1)} %get-tuple-element.20), channel_id=1, source_target_pairs={{0,2},{1,3},{2,0},{3,1},{4,6},{5,7},{6,4},{7,5},{8,10},{9,11},{10,... | collective-permute-start | bytes 442376 | tf_op jit(solution)/shard_map/ppermute | solution.py:271
  66.2 9.5 %collective-permute-start.20 = (f32[1,48,768]{2,1,0:T(8,128)S(1)}, f32[1,48,768]{2,1,0:T(8,128)S(1)}, u32[]{:S(2)}, u32[]{:S(2)}) collective-permute-start(f32[1,48,768]{2,1,0:T(8,128)S(1)} %get-tuple-element.28), channel_id=1, source_target_pairs={{0,2},{1,3},{2,0},{3,1},{4,6},{5,7},{6,4},{7,5},{8,10},{9,11},{10,... | collective-permute-start | bytes 442376 | tf_op jit(solution)/shard_map/ppermute | solution.py:271
  78.6 1.9 %collective-permute-start.21 = (bf16[2,48,768]{2,1,0:T(8,128)(2,1)S(1)}, bf16[2,48,768]{2,1,0:T(8,128)(2,1)S(1)}, u32[]{:S(2)}, u32[]{:S(2)}) collective-permute-start(bf16[2,48,768]{2,1,0:T(8,128)(2,1)S(1)} %get-tuple-element.30), channel_id=1, source_target_pairs={{0,1},{1,0},{2,3},{3,2},{4,5},{5,4},{6,7},{7,6},{8,9},{9,8},{10,11... | collective-permute-start | bytes 442376 | tf_op jit(solution)/shard_map/ppermute | solution.py:277
  78.7 6.8 %collective-permute-start.22 = (bf16[2,48,768]{2,1,0:T(8,128)(2,1)S(1)}, bf16[2,48,768]{2,1,0:T(8,128)(2,1)S(1)}, u32[]{:S(2)}, u32[]{:S(2)}) collective-permute-start(bf16[2,48,768]{2,1,0:T(8,128)(2,1)S(1)} %get-tuple-element.31), channel_id=1, source_target_pairs={{0,2},{1,3},{2,0},{3,1},{4,6},{5,7},{6,4},{7,5},{8,10},{9,11},{10,... | collective-permute-start | bytes 442376 | tf_op jit(solution)/shard_map/ppermute | solution.py:277
  80.3 7.3 %collective-permute-start.23 = (bf16[2,48,768]{2,1,0:T(8,128)(2,1)S(1)}, bf16[2,48,768]{2,1,0:T(8,128)(2,1)S(1)}, u32[]{:S(2)}, u32[]{:S(2)}) collective-permute-start(bf16[2,48,768]{2,1,0:T(8,128)(2,1)S(1)} %get-tuple-element.32), channel_id=1, source_target_pairs={{0,3},{1,2},{2,1},{3,0},{4,7},{5,6},{6,5},{7,4},{8,11},{9,10},{10,... | collective-permute-start | bytes 442376 | tf_op jit(solution)/shard_map/ppermute | solution.py:277
where the time goes:
time: 88.9 us; the launch traced here: 88.7 us
  starting transfers between devices  32.9 us (37%)
  waiting for transfers between devices  31.5 us (35%)
  Pallas kernels  20.1 us (23%)
  local copies, waits for them, and re-layouts  4.1 us (5%)
    pallas_call x5, Pallas kernels, multiply(): pl.pallas_call(functools.partial(multiply_kernel, offsets, n, npcol, widt...  15.5 us
    ppermute x3, waiting for transfers between devices, ring_body(): a_down.append(lax.ppermute(a_down[-1], 'prow', down))  8.71 us
    ppermute x3, starting transfers between devices, ring_body(): a_up.append(lax.ppermute(a_up[-1], 'prow', up))  7.91 us
    ppermute x5, waiting for transfers between devices, ring_body(): got = lax.ppermute(send, 'pcol', across)  7.34 us
    ppermute x3, waiting for transfers between devices, ring_body(): parts.append(lax.ppermute(send, 'pcol', [(c, c ^ j) for c in range(npcol)]))  7.02 us
    ppermute x3, starting transfers between devices, ring_body(): b_down.append(lax.ppermute(b_down[-1], 'prow', down))  6.81 us
    ppermute x5, starting transfers between devices, ring_body(): got = lax.ppermute(send, 'pcol', across)  5.87 us
    ppermute x3, starting transfers between devices, ring_body(): a_down.append(lax.ppermute(a_down[-1], 'prow', down))  5.51 us
  transfers between devices with their start and end apart: 24, of which 13 were waited for; matrix products, arithmetic and copies ran while one was open for 1% of the time, Pallas kernels for 20%

commit v1 on v0

--- a/solution.py
+++ b/solution.py
@@ -84,38 +84,38 @@
     col = lax.axis_index("pcol")
     pos = ring_pos(lax.axis_index("prow"), n)
 
-    @pl.when(pl.program_id(0) == 0)
-    def _():
-        for u, offset in enumerate(offsets):
-            row = ring_row(lax.rem(pos + offset + n, n), n)
-            masks = owner_masks(widths_ref, row * width + (col % 2) * half, half, groups)
-            for q in range(2):
-                part = col if q == 0 else col + 1 - 2 * (col % 2)
-                for b in range(depth):
-                    keep = keep_of(masks, struct_ref, b * npcol + part).astype(jnp.bfloat16)
-                    for s in range(blk // 128):
-                        at = pl.ds(s * 128, 128)
-                        masked[q * depth + b, pl.ds(u * half, half), at] = (
-                            panels[2 * u + q][b, :, at] * keep
-                        )
-
-    total = None
-    for q, a_ref in enumerate((own_ref, other_ref)):
-        for b in range(depth):
-            term = lax.dot_general(
-                masked[q * depth + b],
-                a_ref[0, b],
-                (((1,), (1,)), ((), ())),
-                preferred_element_type=jnp.float32,
-            )
-            total = term if total is None else total + term
+    for u, offset in enumerate(offsets):
+        row = ring_row(lax.rem(pos + offset + n, n), n)
+        masks = owner_masks(widths_ref, row * width + (col % 2) * half, half, groups)
+        for q in range(2):
+            part = col if q == 0 else col + 1 - 2 * (col % 2)
+            for b in range(depth):
+                keep = keep_of(masks, struct_ref, b * npcol + part).astype(jnp.bfloat16)
+                for s in range(blk // 128):
+                    at = pl.ds(s * 128, 128)
+                    masked[q * depth + b, pl.ds(u * half, half), at] = (
+                        panels[2 * u + q][b, :, at] * keep
+                    )
+
     first = (col // 2) == 0
     part = half // 2
-    for u in range(count):
-        low = total[u * half : u * half + part]
-        high = total[u * half + part : (u + 1) * half]
-        hold_ref[u] = jnp.where(first, low, high)
-        send_ref[u] = jnp.where(first, high, low)
+    for a in range(own_ref.shape[0]):
+        total = None
+        for q, a_ref in enumerate((own_ref, other_ref)):
+            for b in range(depth):
+                term = lax.dot_general(
+                    masked[q * depth + b],
+                    a_ref[a, b],
+                    (((1,), (1,)), ((), ())),
+                    preferred_element_type=jnp.float32,
+                )
+                total = term if total is None else total + term
+        at = pl.ds(a * blk, blk)
+        for u in range(count):
+            low = total[u * half : u * half + part]
+            high = total[u * half + part : (u + 1) * half]
+            hold_ref[u, :, at] = jnp.where(first, low, high)
+            send_ref[u, :, at] = jnp.where(first, high, low)
 
 
 def multiply(offsets, n, npcol, width, structure, widths, panels, own, other):
@@ -123,15 +123,12 @@
     depth, half, blk = panels[0].shape
     rows = own.shape[0]
     shape = jax.ShapeDtypeStruct((count, half // 2, rows * blk), jnp.float32)
-    whole = pl.BlockSpec((depth, half, blk), lambda a: (0, 0, 0))
-    ablock = pl.BlockSpec((1, depth, blk, blk), lambda a: (a, 0, 0, 0))
-    oblock = pl.BlockSpec((count, half // 2, blk), lambda a: (0, 0, a))
+    whole = pl.BlockSpec(memory_space=pltpu.VMEM)
     flops = 2 * count * half * 2 * depth * blk * rows * blk
     return pl.pallas_call(
         functools.partial(multiply_kernel, offsets, n, npcol, width),
-        grid=(rows,),
-        in_specs=[SMEM, SMEM] + [whole] * (2 * count) + [ablock] * 2,
-        out_specs=[oblock, oblock],
+        in_specs=[SMEM, SMEM] + [whole] * (2 * count + 2),
+        out_specs=[whole, whole],
         out_shape=[shape, shape],
         scratch_shapes=[pltpu.VMEM((2 * depth, count * half, blk), jnp.bfloat16)],
         cost_estimate=pl.CostEstimate(
@@ -202,34 +199,38 @@
     )(*parts)
 
 
-def lay_kernel(width, *refs):
+def lay_kernel(n, width, *refs):
     parts, out_ref, store = refs[:-2], refs[-2], refs[-1]
-    count, part, _ = parts[0].shape
-    col = lax.axis_index("pcol")
-    for j, ref in enumerate(parts):
+    early, last = parts[: len(parts) // 2], parts[len(parts) // 2 :]
+    count, part, _ = early[0].shape
+    col = lax.axis_index("pcol")
+    pos = ring_pos(lax.axis_index("prow"), n)
+    for j, (ref, end) in enumerate(zip(early, last)):
         source = col ^ j
         start = (source % 2) * 2 * part + (source // 2) * part
         for y in range(count):
             at = pl.multiple_of(y * width + start, 16)
-            store[pl.ds(at, part), :] = ref[y].astype(jnp.float32)
+            is_last = lax.rem(ring_pos(2 * col + y, n) - pos + n, n) == n // 2
+            value = jnp.where(is_last, end[0].astype(jnp.float32), ref[y].astype(jnp.float32))
+            store[pl.ds(at, part), :] = value
     blocks, blk, _ = out_ref.shape
     for a in range(blocks):
         out_ref[a] = store[:, a * blk : (a + 1) * blk].T.astype(jnp.bfloat16)
 
 
-def lay(width, blocks, parts):
-    whole = pl.BlockSpec(memory_space=pltpu.VMEM)
-    count, _, height = parts[0].shape
+def lay(n, width, blocks, early, last):
+    whole = pl.BlockSpec(memory_space=pltpu.VMEM)
+    count, _, height = early[0].shape
     columns = count * width
     return pl.pallas_call(
-        functools.partial(lay_kernel, width),
-        in_specs=[whole] * len(parts),
+        functools.partial(lay_kernel, n, width),
+        in_specs=[whole] * (len(early) + len(last)),
         out_specs=whole,
         out_shape=jax.ShapeDtypeStruct((blocks, height // blocks, columns), jnp.bfloat16),
         scratch_shapes=[pltpu.VMEM((columns, height), jnp.float32)],
         compiler_params=pltpu.CompilerParams(vmem_limit_bytes=8 << 20),
         name="lay",
-    )(*parts)
+    )(*early, *last)
 
 
 def ring_body(ainv, panel, structure, widths):
@@ -248,7 +249,8 @@
     own = jnp.transpose(ainv, (0, 1, 3, 4, 2, 5))[:, 0, :, 0]
     cols = jnp.transpose(panel, (0, 1, 3, 2))[:, 0]
     mine = lax.dynamic_slice_in_dim(cols, core * half, half, 1)
-    theirs = lax.dynamic_slice_in_dim(cols, (1 - core) * half, half, 1)
+    later, _ = lax.optimization_barrier((cols, mine))
+    theirs = lax.dynamic_slice_in_dim(later, (1 - core) * half, half, 1)
     partner = lax.ppermute(theirs, "pcol", side)
     other = lax.ppermute(own, "pcol", side)
     a_up, a_down, b_up, b_down = [mine], [mine], [partner], [partner]
@@ -271,11 +273,15 @@
         got = lax.ppermute(send, "pcol", across)
         done.append(finish(offsets, n, width, structure, widths, hold, got))
 
-    kept, *sends = pick([o for o, _ in stages], n, npcol, done)
-    parts = [kept]
+    kept, *sends = pick([o for o, _ in stages[:-1]], n, npcol, done[:-1])
+    early, last = [kept], [done[-1]]
     for j, send in enumerate(sends, 1):
-        parts.append(lax.ppermute(send, "pcol", [(c, c ^ j) for c in range(npcol)]))
-    out = lay(width, own.shape[0], parts)
+        early.append(lax.ppermute(send, "pcol", [(c, c ^ j) for c in range(npcol)]))
+    for j in range(1, npcol):
+        ends = [(r, ring[(ring.index(r) + half_way) % n] // 2) for r in range(n)]
+        perm = [(r * npcol + (to ^ j), r * npcol + to) for r, to in ends]
+        last.append(lax.ppermute(done[-1], ("prow", "pcol"), perm))
+    out = lay(n, width, own.shape[0], early, last)
     return out[:, None]
 
 

time: 88.9 us -> 89.9 us (1.011)
  starting transfers between devices: 32.9 us -> 38.3 us
  Pallas kernels: 20.1 us -> 16.1 us
    ppermute x3 -> x6, starting transfers between devices: 1.92 us -> 7.61 us  [the longest x3 5.56 us: ring_body(): last.append(lax.ppermute(done[-1], ('prow', 'pcol'), perm))]
    pallas_call x5, Pallas kernels: 15.5 us -> 11.4 us  [multiply(): pl.pallas_call(functools.partial(multiply_kernel, offsets, n, npcol, widt...]
    ppermute x3 -> x6, waiting for transfers between devices: 7.02 us -> 3.49 us  [the longest x3 3.48 us: ring_body(): last.append(lax.ppermute(done[-1], ('prow', 'pcol'), perm))]
    ppermute x5, waiting for transfers between devices: 7.34 us -> 9.82 us  [ring_body(): got = lax.ppermute(send, 'pcol', across)]
    dynamic_slice x1 -> x2, local copies, waits for them, and re-layouts: 1.09 us -> 0.05 us  [the longest x1 0.03 us: ring_body(): theirs = lax.dynamic_slice_in_dim(later, (1 - core) * half, half, 1)]
    unnamed x8 -> x10, local copies, waits for them, and re-layouts: 3.01 us -> 3.58 us
  transfers between devices with their start and end apart: 24 -> 27, of which waited for: 13 -> 12; matrix products, arithmetic and copies ran while one was open for 1% -> 0% of each run, Pallas kernels for 20% -> 17%
where the time goes in v1:
time: 89.9 us; the launch traced here: 89.4 us
  starting transfers between devices  38.3 us (43%)
  waiting for transfers between devices  31.1 us (35%)
  Pallas kernels  16.1 us (18%)
  local copies, waits for them, and re-layouts  3.63 us (4%)
    pallas_call x5, Pallas kernels, multiply(): pl.pallas_call(functools.partial(multiply_kernel, offsets, n, npcol, widt...  11.4 us
    ppermute x5, waiting for transfers between devices, ring_body(): got = lax.ppermute(send, 'pcol', across)  9.82 us
    ppermute x3, waiting for transfers between devices, ring_body(): a_down.append(lax.ppermute(a_down[-1], 'prow', down))  8.71 us
    ppermute x3, starting transfers between devices, ring_body(): a_up.append(lax.ppermute(a_up[-1], 'prow', up))  7.22 us
    ppermute x3, starting transfers between devices, ring_body(): b_down.append(lax.ppermute(b_down[-1], 'prow', down))  6.81 us
    ppermute x5, starting transfers between devices, ring_body(): got = lax.ppermute(send, 'pcol', across)  5.86 us
    ppermute x3, waiting for transfers between devices, ring_body(): b_down.append(lax.ppermute(b_down[-1], 'prow', down))  5.63 us
    ppermute x3, starting transfers between devices, ring_body(): last.append(lax.ppermute(done[-1], ('prow', 'pcol'), perm))  5.56 us
  transfers between devices with their start and end apart: 27, of which 12 were waited for; matrix products, arithmetic and copies ran while one was open for 0% of the time, Pallas kernels for 17%

profile of v1, /device:TPU:0, one launch (start us, length us, event | category | flops | bytes accessed | tf_op | source)
XLA Modules:
  0.0 89.4 jit_solution(8676672294973680385)
XLA Ops:
  0.0 0.5 collective-permute-start.1
  0.5 0.6 copy-done
  1.1 0.6 collective-permute-start
  1.7 2.6 %collective-permute-start.3 = (bf16[6,96,256]{2,1,0:T(8,128)(2,1)S(1)}, bf16[6,96,256]{2,1,0:T(8,128)(2,1)S(1)}, u32[]{:S(2)}, u32[]{:S(2)}) collective-permute-start(bf16[6,96,256]{2,1,0:T(8,128)(2,1)S(1)} %dynamic-slice_bitcast_fusion.refs_0_), channel_id=1, source_target_pairs={{0,8},{8,16},{16,24},{24,28},{28,20},{20,12},{12,4},{4,0},{1,9},{9... | collective-permute-start | bytes 884744 | tf_op jit(solution)/shard_map/ppermute | solution.py:258
  4.3 1.0 %collective-permute-done.refs_1_ = bf16[6,96,256]{2,1,0:T(8,128)(2,1)S(1)} collective-permute-done((bf16[6,96,256]{2,1,0:T(8,128)(2,1)S(1)}, bf16[6,96,256]{2,1,0:T(8,128)(2,1)S(1)}, u32[]{:S(2)}, u32[]{:S(2)}) %collective-permute-start) | collective-permute-done | bytes 294944 | tf_op jit(solution)/shard_map/ppermute | solution.py:254
  5.3 2.9 %collective-permute-start.6 = (bf16[6,96,256]{2,1,0:T(8,128)(2,1)S(1)}, bf16[6,96,256]{2,1,0:T(8,128)(2,1)S(1)}, u32[]{:S(2)}, u32[]{:S(2)}) collective-permute-start(bf16[6,96,256]{2,1,0:T(8,128)(2,1)S(1)} %collective-permute-done.refs_1_), channel_id=1, source_target_pairs={{8,0},{16,8},{24,16},{28,24},{20,28},{12,20},{4,12},{0,4},{9,1},{1... | collective-permute-start | bytes 884744 | tf_op jit(solution)/shard_map/ppermute | solution.py:261
  8.2 1.6 %collective-permute-start.5 = (bf16[6,96,256]{2,1,0:T(8,128)(2,1)S(1)}, bf16[6,96,256]{2,1,0:T(8,128)(2,1)S(1)}, u32[]{:S(2)}, u32[]{:S(2)}) collective-permute-start(bf16[6,96,256]{2,1,0:T(8,128)(2,1)S(1)} %dynamic-slice_bitcast_fusion.refs_0_), channel_id=1, source_target_pairs={{8,0},{16,8},{24,16},{28,24},{20,28},{12,20},{4,12},{0,4},{9,1},{1... | collective-permute-start | bytes 884744 | tf_op jit(solution)/shard_map/ppermute | solution.py:259
  9.7 0.4 collective-permute-start.4
  10.2 1.7 %collective-permute-done.3.refs_0_ = bf16[6,96,256]{2,1,0:T(8,128)(2,1)S(1)} collective-permute-done((bf16[6,96,256]{2,1,0:T(8,128)(2,1)S(1)}, bf16[6,96,256]{2,1,0:T(8,128)(2,1)S(1)}, u32[]{:S(2)}, u32[]{:S(2)}) %collective-permute-start.3) | collective-permute-done | bytes 294944 | tf_op jit(solution)/shard_map/ppermute | solution.py:258
  11.9 2.3 %collective-permute-start.8 = (bf16[6,96,256]{2,1,0:T(8,128)(2,1)S(1)}, bf16[6,96,256]{2,1,0:T(8,128)(2,1)S(1)}, u32[]{:S(2)}, u32[]{:S(2)}) collective-permute-start(bf16[6,96,256]{2,1,0:T(8,128)(2,1)S(1)} %collective-permute-done.3.refs_0_), channel_id=1, source_target_pairs={{0,8},{8,16},{16,24},{24,28},{28,20},{20,12},{12,4},{4,0},{1,9},{9... | collective-permute-start | bytes 884744 | tf_op jit(solution)/shard_map/ppermute | solution.py:258
  14.2 1.9 %collective-permute-done.6.refs_3_ = bf16[6,96,256]{2,1,0:T(8,128)(2,1)S(1)} collective-permute-done((bf16[6,96,256]{2,1,0:T(8,128)(2,1)S(1)}, bf16[6,96,256]{2,1,0:T(8,128)(2,1)S(1)}, u32[]{:S(2)}, u32[]{:S(2)}) %collective-permute-start.6) | collective-permute-done | bytes 294944 | tf_op jit(solution)/shard_map/ppermute | solution.py:261
  16.1 2.0 %collective-permute-start.11 = (bf16[6,96,256]{2,1,0:T(8,128)(2,1)S(1)}, bf16[6,96,256]{2,1,0:T(8,128)(2,1)S(1)}, u32[]{:S(2)}, u32[]{:S(2)}) collective-permute-start(bf16[6,96,256]{2,1,0:T(8,128)(2,1)S(1)} %collective-permute-done.6.refs_3_), channel_id=1, source_target_pairs={{8,0},{16,8},{24,16},{28,24},{20,28},{12,20},{4,12},{0,4},{9,1},{1... | collective-permute-start | bytes 884744 | tf_op jit(solution)/shard_map/ppermute | solution.py:261
  18.0 4.4 %collective-permute-done.5.refs_2_ = bf16[6,96,256]{2,1,0:T(8,128)(2,1)S(1)} collective-permute-done((bf16[6,96,256]{2,1,0:T(8,128)(2,1)S(1)}, bf16[6,96,256]{2,1,0:T(8,128)(2,1)S(1)}, u32[]{:S(2)}, u32[]{:S(2)}) %collective-permute-start.5) | collective-permute-done | bytes 294944 | tf_op jit(solution)/shard_map/ppermute | solution.py:259
  22.4 2.0 %collective-permute-start.10 = (bf16[6,96,256]{2,1,0:T(8,128)(2,1)S(1)}, bf16[6,96,256]{2,1,0:T(8,128)(2,1)S(1)}, u32[]{:S(2)}, u32[]{:S(2)}) collective-permute-start(bf16[6,96,256]{2,1,0:T(8,128)(2,1)S(1)} %collective-permute-done.5.refs_2_), channel_id=1, source_target_pairs={{8,0},{16,8},{24,16},{28,24},{20,28},{12,20},{4,12},{0,4},{9,1},{1... | collective-permute-start | bytes 884744 | tf_op jit(solution)/shard_map/ppermute | solution.py:259
  24.4 0.1 collective-permute-start.9
  24.4 0.1 collective-permute-done.8.refs_0_
  24.6 2.3 %collective-permute-start.13 = (bf16[6,96,256]{2,1,0:T(8,128)(2,1)S(1)}, bf16[6,96,256]{2,1,0:T(8,128)(2,1)S(1)}, u32[]{:S(2)}, u32[]{:S(2)}) collective-permute-start(bf16[6,96,256]{2,1,0:T(8,128)(2,1)S(1)} %collective-permute-done.8.refs_0_), channel_id=1, source_target_pairs={{0,8},{8,16},{16,24},{24,28},{28,20},{20,12},{12,4},{4,0},{1,9},{9... | collective-permute-start | bytes 884744 | tf_op jit(solution)/shard_map/ppermute | solution.py:258
  26.8 1.9 %collective-permute-done.11.refs_3_ = bf16[6,96,256]{2,1,0:T(8,128)(2,1)S(1)} collective-permute-done((bf16[6,96,256]{2,1,0:T(8,128)(2,1)S(1)}, bf16[6,96,256]{2,1,0:T(8,128)(2,1)S(1)}, u32[]{:S(2)}, u32[]{:S(2)}) %collective-permute-start.11) | collective-permute-done | bytes 294944 | tf_op jit(solution)/shard_map/ppermute | solution.py:261
  28.7 2.0 %collective-permute-start.16 = (bf16[6,96,256]{2,1,0:T(8,128)(2,1)S(1)}, bf16[6,96,256]{2,1,0:T(8,128)(2,1)S(1)}, u32[]{:S(2)}, u32[]{:S(2)}) collective-permute-start(bf16[6,96,256]{2,1,0:T(8,128)(2,1)S(1)} %collective-permute-done.11.refs_3_), channel_id=1, source_target_pairs={{8,0},{16,8},{24,16},{28,24},{20,28},{12,20},{4,12},{0,4},{9,1},{1... | collective-permute-start | bytes 884744 | tf_op jit(solution)/shard_map/ppermute | solution.py:261
  30.7 4.4 %collective-permute-done.10.refs_2_ = bf16[6,96,256]{2,1,0:T(8,128)(2,1)S(1)} collective-permute-done((bf16[6,96,256]{2,1,0:T(8,128)(2,1)S(1)}, bf16[6,96,256]{2,1,0:T(8,128)(2,1)S(1)}, u32[]{:S(2)}, u32[]{:S(2)}) %collective-permute-start.10) | collective-permute-done | bytes 294944 | tf_op jit(solution)/shard_map/ppermute | solution.py:259
  35.0 2.0 %collective-permute-start.15 = (bf16[6,96,256]{2,1,0:T(8,128)(2,1)S(1)}, bf16[6,96,256]{2,1,0:T(8,128)(2,1)S(1)}, u32[]{:S(2)}, u32[]{:S(2)}) collective-permute-start(bf16[6,96,256]{2,1,0:T(8,128)(2,1)S(1)} %collective-permute-done.10.refs_2_), channel_id=1, source_target_pairs={{8,0},{16,8},{24,16},{28,24},{20,28},{12,20},{4,12},{0,4},{9,1},{1... | collective-permute-start | bytes 884744 | tf_op jit(solution)/shard_map/ppermute | solution.py:259
  37.0 0.1 collective-permute-start.14
  37.1 0.7 collective-permute-done.13.refs_0_
  37.8 1.7 %collective-permute-start.21 = (bf16[6,96,256]{2,1,0:T(8,128)(2,1)S(1)}, bf16[6,96,256]{2,1,0:T(8,128)(2,1)S(1)}, u32[]{:S(2)}, u32[]{:S(2)}) collective-permute-start(bf16[6,96,256]{2,1,0:T(8,128)(2,1)S(1)} %collective-permute-done.13.refs_0_), channel_id=1, source_target_pairs={{0,8},{8,16},{16,24},{24,28},{28,20},{20,12},{12,4},{4,0},{1,9},{9... | collective-permute-start | bytes 884744 | tf_op jit(solution)/shard_map/ppermute | solution.py:262
  39.5 1.9 %collective-permute-done.16.refs_3_ = bf16[6,96,256]{2,1,0:T(8,128)(2,1)S(1)} collective-permute-done((bf16[6,96,256]{2,1,0:T(8,128)(2,1)S(1)}, bf16[6,96,256]{2,1,0:T(8,128)(2,1)S(1)}, u32[]{:S(2)}, u32[]{:S(2)}) %collective-permute-start.16) | collective-permute-done | bytes 294944 | tf_op jit(solution)/shard_map/ppermute | solution.py:261
  41.4 2.0 %collective-permute-start.22 = (bf16[6,96,256]{2,1,0:T(8,128)(2,1)S(1)}, bf16[6,96,256]{2,1,0:T(8,128)(2,1)S(1)}, u32[]{:S(2)}, u32[]{:S(2)}) collective-permute-start(bf16[6,96,256]{2,1,0:T(8,128)(2,1)S(1)} %collective-permute-done.16.refs_3_), channel_id=1, source_target_pairs={{8,0},{16,8},{24,16},{28,24},{20,28},{12,20},{4,12},{0,4},{9,1},{1... | collective-permute-start | bytes 884744 | tf_op jit(solution)/shard_map/ppermute | solution.py:263
  43.3 1.7 %copy-done.1 = bf16[3,1,256,6,1,256]{5,2,4,3,1,0:T(8,128)(2,1)S(1)} copy-done((bf16[3,1,256,6,1,256]{5,2,4,3,1,0:T(8,128)(2,1)S(1)}, bf16[3,1,256,6,1,256]{5,2,4,3,1,0:T(8,128)(2,1)}, u32[]{:S(2)}) %copy-start.1) | copy-done | bytes 2359320
  45.0 0.7 copy-done.3
  45.7 0.7 copy-done.4
  46.3 2.4 %shard_map.47 = (f32[2,48,768]{2,1,0:T(8,128)S(1)}, f32[2,48,768]{2,1,0:T(8,128)S(1)}) custom-call(s32[4,24]{1,0:T(4,128)S(1)} %copy-done.3, s32[4]{0:T(128)S(1)} %copy-done.4, bf16[6,96,256]{2,1,0:T(8,128)(2,1)S(1)} %collective-permute-done.3.refs_0_, bf16[6,96,256]{2,1,0:T(8,128)(2,1)S(1)} %collective-permute-done.4.refs_1_, ...), custom_call_target="tpu_custom_call" | custom-call | flops 905969664 | bytes 5898240 | tf_op jit(solution)/shard_map/pallas_call | solution.py:128
  48.7 1.5 %collective-permute-start.7 = (f32[2,48,768]{2,1,0:T(8,128)S(1)}, f32[2,48,768]{2,1,0:T(8,128)S(1)}, u32[]{:S(2)}, u32[]{:S(2)}) collective-permute-start(f32[2,48,768]{2,1,0:T(8,128)S(1)} %get-tuple-element.24), channel_id=1, source_target_pairs={{0,2},{1,3},{2,0},{3,1},{4,6},{5,7},{6,4},{7,5},{8,10},{9,11},{10,... | collective-permute-start | bytes 884744 | tf_op jit(solution)/shard_map/ppermute | solution.py:273
  50.2 2.4 %shard_map.48 = (f32[2,48,768]{2,1,0:T(8,128)S(1)}, f32[2,48,768]{2,1,0:T(8,128)S(1)}) custom-call(s32[4,24]{1,0:T(4,128)S(1)} %copy-done.3, s32[4]{0:T(128)S(1)} %copy-done.4, bf16[6,96,256]{2,1,0:T(8,128)(2,1)S(1)} %collective-permute-done.8.refs_0_, bf16[6,96,256]{2,1,0:T(8,128)(2,1)S(1)} %collective-permute-done.9.refs_1_, ...), custom_call_target="tpu_custom_call" | custom-call | flops 905969664 | bytes 5898240 | tf_op jit(solution)/shard_map/pallas_call | solution.py:128
  52.6 0.0 collective-permute-done.15.refs_2_
  52.6 0.6 collective-permute-start.12
  53.2 2.4 %shard_map.49 = (f32[2,48,768]{2,1,0:T(8,128)S(1)}, f32[2,48,768]{2,1,0:T(8,128)S(1)}) custom-call(s32[4,24]{1,0:T(4,128)S(1)} %copy-done.3, s32[4]{0:T(128)S(1)} %copy-done.4, bf16[6,96,256]{2,1,0:T(8,128)(2,1)S(1)} %collective-permute-done.13.refs_0_, bf16[6,96,256]{2,1,0:T(8,128)(2,1)S(1)} %collective-permute-done.14.refs_1_, ...), custom_call_target="tpu_custom_call" | custom-call | flops 905969664 | bytes 5898240 | tf_op jit(solution)/shard_map/pallas_call | solution.py:128
  55.6 0.0 copy-start.2
  55.6 1.5 %collective-permute-start.17 = (f32[2,48,768]{2,1,0:T(8,128)S(1)}, f32[2,48,768]{2,1,0:T(8,128)S(1)}, u32[]{:S(2)}, u32[]{:S(2)}) collective-permute-start(f32[2,48,768]{2,1,0:T(8,128)S(1)} %get-tuple-element.28), channel_id=1, source_target_pairs={{0,2},{1,3},{2,0},{3,1},{4,6},{5,7},{6,4},{7,5},{8,10},{9,11},{10,... | collective-permute-start | bytes 884744 | tf_op jit(solution)/shard_map/ppermute | solution.py:273
  57.2 0.0 collective-permute-done.21.refs_0_
  57.2 0.0 collective-permute-done.22.refs_1_
  57.2 2.2 %shard_map.50 = (f32[1,48,768]{2,1,0:T(8,128)S(1)}, f32[1,48,768]{2,1,0:T(8,128)S(1)}) custom-call(s32[4,24]{1,0:T(4,128)S(1)} %copy-done.3, s32[4]{0:T(128)S(1)} %copy-done.4, bf16[6,96,256]{2,1,0:T(8,128)(2,1)S(1)} %collective-permute-done.21.refs_0_, bf16[6,96,256]{2,1,0:T(8,128)(2,1)S(1)} %collective-permute-done.22.refs_1_, ...), custom_call_target="tpu_custom_call" | custom-call | flops 452984832 | bytes 5308416 | tf_op jit(solution)/shard_map/pallas_call | solution.py:128
  59.4 0.6 collective-permute-start.23
  60.0 2.2 %shard_map.46 = (f32[1,48,768]{2,1,0:T(8,128)S(1)}, f32[1,48,768]{2,1,0:T(8,128)S(1)}) custom-call(s32[4,24]{1,0:T(4,128)S(1)} %copy-done.3, s32[4]{0:T(128)S(1)} %copy-done.4, bf16[6,96,256]{2,1,0:T(8,128)(2,1)S(1)} %dynamic-slice_bitcast_fusion.refs_0_, bf16[6,96,256]{2,1,0:T(8,128)(2,1)S(1)} %collective-permute-done.refs_1_, ...), custom_call_target="tpu_custom_call" | custom-call | flops 452984832 | bytes 5308416 | tf_op jit(solution)/shard_map/pallas_call | solution.py:128
  62.1 1.5 %collective-permute-start.2 = (f32[1,48,768]{2,1,0:T(8,128)S(1)}, f32[1,48,768]{2,1,0:T(8,128)S(1)}, u32[]{:S(2)}, u32[]{:S(2)}) collective-permute-start(f32[1,48,768]{2,1,0:T(8,128)S(1)} %get-tuple-element.22), channel_id=1, source_target_pairs={{0,2},{1,3},{2,0},{3,1},{4,6},{5,7},{6,4},{7,5},{8,10},{9,11},{10,... | collective-permute-start | bytes 442376 | tf_op jit(solution)/shard_map/ppermute | solution.py:273
  63.7 9.6 %collective-permute-done.23.got_ref = f32[1,48,768]{2,1,0:T(8,128)S(1)} collective-permute-done((f32[1,48,768]{2,1,0:T(8,128)S(1)}, f32[1,48,768]{2,1,0:T(8,128)S(1)}, u32[]{:S(2)}, u32[]{:S(2)}) %collective-permute-start.23) | collective-permute-done | bytes 147488 | tf_op jit(solution)/shard_map/ppermute | solution.py:273
  73.2 0.6 finish.9.refs_4_
  73.9 0.7 collective-permute-start.24
  74.6 0.3 collective-permute-done.2.got_ref
  74.8 0.6 finish.5.refs_0_
  75.5 0.0 collective-permute-done.7.got_ref
  75.5 0.7 finish.6.refs_1_
  76.2 0.7 finish.7.refs_2_
  76.9 0.7 finish.8.refs_3_
  77.6 0.1 pick.1
  77.7 0.1 collective-permute-start.18
  77.8 1.9 %collective-permute-start.19 = (bf16[2,48,768]{2,1,0:T(8,128)(2,1)S(1)}, bf16[2,48,768]{2,1,0:T(8,128)(2,1)S(1)}, u32[]{:S(2)}, u32[]{:S(2)}) collective-permute-start(bf16[2,48,768]{2,1,0:T(8,128)(2,1)S(1)} %get-tuple-element.31), channel_id=1, source_target_pairs={{0,2},{1,3},{2,0},{3,1},{4,6},{5,7},{6,4},{7,5},{8,10},{9,11},{10,... | collective-permute-start | bytes 442376 | tf_op jit(solution)/shard_map/ppermute | solution.py:279
  79.7 0.0 collective-permute-start.20
  79.8 0.7 collective-permute-start.25
  80.4 0.0 collective-permute-done.24.refs_5_
  80.4 4.2 %collective-permute-start.26 = (bf16[1,48,768]{2,1,0:T(8,128)(2,1)S(1)}, bf16[1,48,768]{2,1,0:T(8,128)(2,1)S(1)}, u32[]{:S(2)}, u32[]{:S(2)}) collective-permute-start(bf16[1,48,768]{2,1,0:T(8,128)(2,1)S(1)} %finish.9.refs_4_), channel_id=1, source_target_pairs={{0,3},{4,7},{9,10},{13,14},{18,17},{22,21},{27,24},{31,28}} | collective-permute-start | bytes 221192 | tf_op jit(solution)/shard_map/ppermute | solution.py:283
  84.7 0.0 collective-permute-done.25.refs_6_
  84.7 3.5 %collective-permute-done.26.refs_7_ = bf16[1,48,768]{2,1,0:T(8,128)(2,1)S(1)} collective-permute-done((bf16[1,48,768]{2,1,0:T(8,128)(2,1)S(1)}, bf16[1,48,768]{2,1,0:T(8,128)(2,1)S(1)}, u32[]{:S(2)}, u32[]{:S(2)}) %collective-permute-start.26) | collective-permute-done | bytes 73760 | tf_op jit(solution)/shard_map/ppermute | solution.py:283
  88.2 0.0 collective-permute-done.18.refs_1_
  88.2 0.0 collective-permute-done.19.refs_2_
  88.2 1.2 %lay.1 = bf16[3,256,384]{2,1,0:T(8,128)(2,1)} custom-call(bf16[2,48,768]{2,1,0:T(8,128)(2,1)S(1)} %get-tuple-element.29.refs_0_, bf16[2,48,768]{2,1,0:T(8,128)(2,1)S(1)} %collective-permute-done.18.refs_1_, bf16[2,48,768]{2,1,0:T(8,128)(2,1)S(1)} %collective-permute-done.19.refs_2_, bf16[2,48,768]{2,1,0:T(8,128)(2,1)S(1)} %collective-permute-done.20.refs_3_, ...), custom_call_target="tpu_custom_call" | custom-call | tf_op jit(solution)/shard_map/lay/pallas_call | solution.py:225
  (14 shorter events, 0.1 us)
Async XLA Ops:
  0.0 1.1 %copy-start = (bf16[6,1,256,192]{2,3,1,0:T(8,128)(2,1)S(1)}, bf16[6,1,256,192]{2,3,1,0:T(8,128)(2,1)}, u32[]{:S(2)}) copy-start(bf16[6,1,256,192]{2,3,1,0:T(8,128)(2,1)} %param.5) | copy-start | bytes 1769476
  0.0 43.3 %collective-permute-start.1 = (bf16[3,6,256,256]{3,2,1,0:T(8,128)(2,1)}, bf16[3,6,256,256]{3,2,1,0:T(8,128)(2,1)S(1)}, u32[]{:S(2)}, u32[]{:S(2)}) collective-permute-start(bf16[3,6,256,256]{3,2,1,0:T(8,128)(2,1)} %bitcast.19), channel_id=1, source_target_pairs={{0,1},{1,0},{2,3},{3,2},{4,5},{5,4},{6,7},{7,6},{8,9},{9,8},{10,11... | collective-permute-start | bytes 7077896 | tf_op jit(solution)/shard_map/ppermute | solution.py:255
  1.1 4.2 %collective-permute-start = (bf16[6,96,256]{2,1,0:T(8,128)(2,1)S(1)}, bf16[6,96,256]{2,1,0:T(8,128)(2,1)S(1)}, u32[]{:S(2)}, u32[]{:S(2)}) collective-permute-start(bf16[6,96,256]{2,1,0:T(8,128)(2,1)S(1)} %constant_dynamic-slice_fusion), channel_id=1, source_target_pairs={{0,1},{1,0},{2,3},{3,2},{4,5},{5,4},{6,7},{7,6},{8,9},{9,8},{10,11... | collective-permute-start | bytes 884744 | tf_op jit(solution)/shard_map/ppermute | solution.py:254
  1.7 10.2 %collective-permute-start.3 = (bf16[6,96,256]{2,1,0:T(8,128)(2,1)S(1)}, bf16[6,96,256]{2,1,0:T(8,128)(2,1)S(1)}, u32[]{:S(2)}, u32[]{:S(2)}) collective-permute-start(bf16[6,96,256]{2,1,0:T(8,128)(2,1)S(1)} %dynamic-slice_bitcast_fusion.refs_0_), channel_id=1, source_target_pairs={{0,8},{8,16},{16,24},{24,28},{28,20},{20,12},{12,4},{4,0},{1,9},{9... | collective-permute-start | bytes 884744 | tf_op jit(solution)/shard_map/ppermute | solution.py:258
  5.3 10.8 %collective-permute-start.6 = (bf16[6,96,256]{2,1,0:T(8,128)(2,1)S(1)}, bf16[6,96,256]{2,1,0:T(8,128)(2,1)S(1)}, u32[]{:S(2)}, u32[]{:S(2)}) collective-permute-start(bf16[6,96,256]{2,1,0:T(8,128)(2,1)S(1)} %collective-permute-done.refs_1_), channel_id=1, source_target_pairs={{8,0},{16,8},{24,16},{28,24},{20,28},{12,20},{4,12},{0,4},{9,1},{1... | collective-permute-start | bytes 884744 | tf_op jit(solution)/shard_map/ppermute | solution.py:261
  8.2 14.2 %collective-permute-start.5 = (bf16[6,96,256]{2,1,0:T(8,128)(2,1)S(1)}, bf16[6,96,256]{2,1,0:T(8,128)(2,1)S(1)}, u32[]{:S(2)}, u32[]{:S(2)}) collective-permute-start(bf16[6,96,256]{2,1,0:T(8,128)(2,1)S(1)} %dynamic-slice_bitcast_fusion.refs_0_), channel_id=1, source_target_pairs={{8,0},{16,8},{24,16},{28,24},{20,28},{12,20},{4,12},{0,4},{9,1},{1... | collective-permute-start | bytes 884744 | tf_op jit(solution)/shard_map/ppermute | solution.py:259
  9.7 14.6 %collective-permute-start.4 = (bf16[6,96,256]{2,1,0:T(8,128)(2,1)S(1)}, bf16[6,96,256]{2,1,0:T(8,128)(2,1)S(1)}, u32[]{:S(2)}, u32[]{:S(2)}) collective-permute-start(bf16[6,96,256]{2,1,0:T(8,128)(2,1)S(1)} %collective-permute-done.refs_1_), channel_id=1, source_target_pairs={{0,8},{8,16},{16,24},{24,28},{28,20},{20,12},{12,4},{4,0},{1,9},{9... | collective-permute-start | bytes 884744 | tf_op jit(solution)/shard_map/ppermute | solution.py:260
  11.9 12.7 %collective-permute-start.8 = (bf16[6,96,256]{2,1,0:T(8,128)(2,1)S(1)}, bf16[6,96,256]{2,1,0:T(8,128)(2,1)S(1)}, u32[]{:S(2)}, u32[]{:S(2)}) collective-permute-start(bf16[6,96,256]{2,1,0:T(8,128)(2,1)S(1)} %collective-permute-done.3.refs_0_), channel_id=1, source_target_pairs={{0,8},{8,16},{16,24},{24,28},{28,20},{20,12},{12,4},{4,0},{1,9},{9... | collective-permute-start | bytes 884744 | tf_op jit(solution)/shard_map/ppermute | solution.py:258
  16.1 12.6 %collective-permute-start.11 = (bf16[6,96,256]{2,1,0:T(8,128)(2,1)S(1)}, bf16[6,96,256]{2,1,0:T(8,128)(2,1)S(1)}, u32[]{:S(2)}, u32[]{:S(2)}) collective-permute-start(bf16[6,96,256]{2,1,0:T(8,128)(2,1)S(1)} %collective-permute-done.6.refs_3_), channel_id=1, source_target_pairs={{8,0},{16,8},{24,16},{28,24},{20,28},{12,20},{4,12},{0,4},{9,1},{1... | collective-permute-start | bytes 884744 | tf_op jit(solution)/shard_map/ppermute | solution.py:261
  22.4 12.6 %collective-permute-start.10 = (bf16[6,96,256]{2,1,0:T(8,128)(2,1)S(1)}, bf16[6,96,256]{2,1,0:T(8,128)(2,1)S(1)}, u32[]{:S(2)}, u32[]{:S(2)}) collective-permute-start(bf16[6,96,256]{2,1,0:T(8,128)(2,1)S(1)} %collective-permute-done.5.refs_2_), channel_id=1, source_target_pairs={{8,0},{16,8},{24,16},{28,24},{20,28},{12,20},{4,12},{0,4},{9,1},{1... | collective-permute-start | bytes 884744 | tf_op jit(solution)/shard_map/ppermute | solution.py:259
  24.4 12.6 %collective-permute-start.9 = (bf16[6,96,256]{2,1,0:T(8,128)(2,1)S(1)}, bf16[6,96,256]{2,1,0:T(8,128)(2,1)S(1)}, u32[]{:S(2)}, u32[]{:S(2)}) collective-permute-start(bf16[6,96,256]{2,1,0:T(8,128)(2,1)S(1)} %collective-permute-done.4.refs_1_), channel_id=1, source_target_pairs={{0,8},{8,16},{16,24},{24,28},{28,20},{20,12},{12,4},{4,0},{1,9},{9... | collective-permute-start | bytes 884744 | tf_op jit(solution)/shard_map/ppermute | solution.py:260
  24.6 13.2 %collective-permute-start.13 = (bf16[6,96,256]{2,1,0:T(8,128)(2,1)S(1)}, bf16[6,96,256]{2,1,0:T(8,128)(2,1)S(1)}, u32[]{:S(2)}, u32[]{:S(2)}) collective-permute-start(bf16[6,96,256]{2,1,0:T(8,128)(2,1)S(1)} %collective-permute-done.8.refs_0_), channel_id=1, source_target_pairs={{0,8},{8,16},{16,24},{24,28},{28,20},{20,12},{12,4},{4,0},{1,9},{9... | collective-permute-start | bytes 884744 | tf_op jit(solution)/shard_map/ppermute | solution.py:258
  28.7 12.6 %collective-permute-start.16 = (bf16[6,96,256]{2,1,0:T(8,128)(2,1)S(1)}, bf16[6,96,256]{2,1,0:T(8,128)(2,1)S(1)}, u32[]{:S(2)}, u32[]{:S(2)}) collective-permute-start(bf16[6,96,256]{2,1,0:T(8,128)(2,1)S(1)} %collective-permute-done.11.refs_3_), channel_id=1, source_target_pairs={{8,0},{16,8},{24,16},{28,24},{20,28},{12,20},{4,12},{0,4},{9,1},{1... | collective-permute-start | bytes 884744 | tf_op jit(solution)/shard_map/ppermute | solution.py:261
  35.0 17.6 %collective-permute-start.15 = (bf16[6,96,256]{2,1,0:T(8,128)(2,1)S(1)}, bf16[6,96,256]{2,1,0:T(8,128)(2,1)S(1)}, u32[]{:S(2)}, u32[]{:S(2)}) collective-permute-start(bf16[6,96,256]{2,1,0:T(8,128)(2,1)S(1)} %collective-permute-done.10.refs_2_), channel_id=1, source_target_pairs={{8,0},{16,8},{24,16},{28,24},{20,28},{12,20},{4,12},{0,4},{9,1},{1... | collective-permute-start | bytes 884744 | tf_op jit(solution)/shard_map/ppermute | solution.py:259
  37.0 16.2 %collective-permute-start.14 = (bf16[6,96,256]{2,1,0:T(8,128)(2,1)S(1)}, bf16[6,96,256]{2,1,0:T(8,128)(2,1)S(1)}, u32[]{:S(2)}, u32[]{:S(2)}) collective-permute-start(bf16[6,96,256]{2,1,0:T(8,128)(2,1)S(1)} %collective-permute-done.9.refs_1_), channel_id=1, source_target_pairs={{0,8},{8,16},{16,24},{24,28},{28,20},{20,12},{12,4},{4,0},{1,9},{9... | collective-permute-start | bytes 884744 | tf_op jit(solution)/shard_map/ppermute | solution.py:260
  37.8 19.4 %collective-permute-start.21 = (bf16[6,96,256]{2,1,0:T(8,128)(2,1)S(1)}, bf16[6,96,256]{2,1,0:T(8,128)(2,1)S(1)}, u32[]{:S(2)}, u32[]{:S(2)}) collective-permute-start(bf16[6,96,256]{2,1,0:T(8,128)(2,1)S(1)} %collective-permute-done.13.refs_0_), channel_id=1, source_target_pairs={{0,8},{8,16},{16,24},{24,28},{28,20},{20,12},{12,4},{4,0},{1,9},{9... | collective-permute-start | bytes 884744 | tf_op jit(solution)/shard_map/ppermute | solution.py:262
  41.4 15.8 %collective-permute-start.22 = (bf16[6,96,256]{2,1,0:T(8,128)(2,1)S(1)}, bf16[6,96,256]{2,1,0:T(8,128)(2,1)S(1)}, u32[]{:S(2)}, u32[]{:S(2)}) collective-permute-start(bf16[6,96,256]{2,1,0:T(8,128)(2,1)S(1)} %collective-permute-done.16.refs_3_), channel_id=1, source_target_pairs={{8,0},{16,8},{24,16},{28,24},{20,28},{12,20},{4,12},{0,4},{9,1},{1... | collective-permute-start | bytes 884744 | tf_op jit(solution)/shard_map/ppermute | solution.py:263
  43.3 1.7 %copy-start.1 = (bf16[3,1,256,6,1,256]{5,2,4,3,1,0:T(8,128)(2,1)S(1)}, bf16[3,1,256,6,1,256]{5,2,4,3,1,0:T(8,128)(2,1)}, u32[]{:S(2)}) copy-start(bf16[3,1,256,6,1,256]{5,2,4,3,1,0:T(8,128)(2,1)} %param.4) | copy-start | bytes 7077892
  45.0 0.7 copy-start.3
  45.7 0.7 copy-start.4
  48.7 26.8 %collective-permute-start.7 = (f32[2,48,768]{2,1,0:T(8,128)S(1)}, f32[2,48,768]{2,1,0:T(8,128)S(1)}, u32[]{:S(2)}, u32[]{:S(2)}) collective-permute-start(f32[2,48,768]{2,1,0:T(8,128)S(1)} %get-tuple-element.24), channel_id=1, source_target_pairs={{0,2},{1,3},{2,0},{3,1},{4,6},{5,7},{6,4},{7,5},{8,10},{9,11},{10,... | collective-permute-start | bytes 884744 | tf_op jit(solution)/shard_map/ppermute | solution.py:273
  52.6 23.6 %collective-permute-start.12 = (f32[2,48,768]{2,1,0:T(8,128)S(1)}, f32[2,48,768]{2,1,0:T(8,128)S(1)}, u32[]{:S(2)}, u32[]{:S(2)}) collective-permute-start(f32[2,48,768]{2,1,0:T(8,128)S(1)} %get-tuple-element.26), channel_id=1, source_target_pairs={{0,2},{1,3},{2,0},{3,1},{4,6},{5,7},{6,4},{7,5},{8,10},{9,11},{10,... | collective-permute-start | bytes 884744 | tf_op jit(solution)/shard_map/ppermute | solution.py:273
  55.6 4.4 %copy-start.2 = (bf16[3,1,256,6,1,256]{5,2,4,3,1,0:T(8,128)(2,1)S(1)}, bf16[3,1,256,6,1,256]{5,2,4,3,1,0:T(8,128)(2,1)}, u32[]{:S(2)}) copy-start(bf16[3,1,256,6,1,256]{5,2,4,3,1,0:T(8,128)(2,1)} %param.4) | copy-start | bytes 7077892
  55.6 21.3 %collective-permute-start.17 = (f32[2,48,768]{2,1,0:T(8,128)S(1)}, f32[2,48,768]{2,1,0:T(8,128)S(1)}, u32[]{:S(2)}, u32[]{:S(2)}) collective-permute-start(f32[2,48,768]{2,1,0:T(8,128)S(1)} %get-tuple-element.28), channel_id=1, source_target_pairs={{0,2},{1,3},{2,0},{3,1},{4,6},{5,7},{6,4},{7,5},{8,10},{9,11},{10,... | collective-permute-start | bytes 884744 | tf_op jit(solution)/shard_map/ppermute | solution.py:273
  59.4 13.9 %collective-permute-start.23 = (f32[1,48,768]{2,1,0:T(8,128)S(1)}, f32[1,48,768]{2,1,0:T(8,128)S(1)}, u32[]{:S(2)}, u32[]{:S(2)}) collective-permute-start(f32[1,48,768]{2,1,0:T(8,128)S(1)} %get-tuple-element.34), channel_id=1, source_target_pairs={{0,2},{1,3},{2,0},{3,1},{4,6},{5,7},{6,4},{7,5},{8,10},{9,11},{10,... | collective-permute-start | bytes 442376 | tf_op jit(solution)/shard_map/ppermute | solution.py:273
  62.1 12.7 %collective-permute-start.2 = (f32[1,48,768]{2,1,0:T(8,128)S(1)}, f32[1,48,768]{2,1,0:T(8,128)S(1)}, u32[]{:S(2)}, u32[]{:S(2)}) collective-permute-start(f32[1,48,768]{2,1,0:T(8,128)S(1)} %get-tuple-element.22), channel_id=1, source_target_pairs={{0,2},{1,3},{2,0},{3,1},{4,6},{5,7},{6,4},{7,5},{8,10},{9,11},{10,... | collective-permute-start | bytes 442376 | tf_op jit(solution)/shard_map/ppermute | solution.py:273
  73.9 6.6 %collective-permute-start.24 = (bf16[1,48,768]{2,1,0:T(8,128)(2,1)S(1)}, bf16[1,48,768]{2,1,0:T(8,128)(2,1)S(1)}, u32[]{:S(2)}, u32[]{:S(2)}) collective-permute-start(bf16[1,48,768]{2,1,0:T(8,128)(2,1)S(1)} %finish.9.refs_4_), channel_id=1, source_target_pairs={{2,3},{6,7},{11,10},{15,14},{16,17},{20,21},{25,24},{29,28}} | collective-permute-start | bytes 221192 | tf_op jit(solution)/shard_map/ppermute | solution.py:283
  77.7 10.5 %collective-permute-start.18 = (bf16[2,48,768]{2,1,0:T(8,128)(2,1)S(1)}, bf16[2,48,768]{2,1,0:T(8,128)(2,1)S(1)}, u32[]{:S(2)}, u32[]{:S(2)}) collective-permute-start(bf16[2,48,768]{2,1,0:T(8,128)(2,1)S(1)} %get-tuple-element.30), channel_id=1, source_target_pairs={{0,1},{1,0},{2,3},{3,2},{4,5},{5,4},{6,7},{7,6},{8,9},{9,8},{10,11... | collective-permute-start | bytes 442376 | tf_op jit(solution)/shard_map/ppermute | solution.py:279
  77.8 10.4 %collective-permute-start.19 = (bf16[2,48,768]{2,1,0:T(8,128)(2,1)S(1)}, bf16[2,48,768]{2,1,0:T(8,128)(2,1)S(1)}, u32[]{:S(2)}, u32[]{:S(2)}) collective-permute-start(bf16[2,48,768]{2,1,0:T(8,128)(2,1)S(1)} %get-tuple-element.31), channel_id=1, source_target_pairs={{0,2},{1,3},{2,0},{3,1},{4,6},{5,7},{6,4},{7,5},{8,10},{9,11},{10,... | collective-permute-start | bytes 442376 | tf_op jit(solution)/shard_map/ppermute | solution.py:279
  79.7 8.5 %collective-permute-start.20 = (bf16[2,48,768]{2,1,0:T(8,128)(2,1)S(1)}, bf16[2,48,768]{2,1,0:T(8,128)(2,1)S(1)}, u32[]{:S(2)}, u32[]{:S(2)}) collective-permute-start(bf16[2,48,768]{2,1,0:T(8,128)(2,1)S(1)} %get-tuple-element.32), channel_id=1, source_target_pairs={{0,3},{1,2},{2,1},{3,0},{4,7},{5,6},{6,5},{7,4},{8,11},{9,10},{10,... | collective-permute-start | bytes 442376 | tf_op jit(solution)/shard_map/ppermute | solution.py:279
  79.8 4.9 %collective-permute-start.25 = (bf16[1,48,768]{2,1,0:T(8,128)(2,1)S(1)}, bf16[1,48,768]{2,1,0:T(8,128)(2,1)S(1)}, u32[]{:S(2)}, u32[]{:S(2)}) collective-permute-start(bf16[1,48,768]{2,1,0:T(8,128)(2,1)S(1)} %finish.9.refs_4_), channel_id=1, source_target_pairs={{1,3},{5,7},{8,10},{12,14},{19,17},{23,21},{26,24},{30,28}} | collective-permute-start | bytes 221192 | tf_op jit(solution)/shard_map/ppermute | solution.py:283
  80.4 7.7 %collective-permute-start.26 = (bf16[1,48,768]{2,1,0:T(8,128)(2,1)S(1)}, bf16[1,48,768]{2,1,0:T(8,128)(2,1)S(1)}, u32[]{:S(2)}, u32[]{:S(2)}) collective-permute-start(bf16[1,48,768]{2,1,0:T(8,128)(2,1)S(1)} %finish.9.refs_4_), channel_id=1, source_target_pairs={{0,3},{4,7},{9,10},{13,14},{18,17},{22,21},{27,24},{31,28}} | collective-permute-start | bytes 221192 | tf_op jit(solution)/shard_map/ppermute | solution.py:283
